TPU v7x, 32 devices: a whole 2x2x4 slice. The times are simulated.
32 devices in a mesh: groups: 2 (over y), dec: 16 (over z, x, core).
Axes of the slice: x: 2, y: 2, z: 4, core: 2. Of those that a mesh axis runs over, the one named last changes fastest.
Arguments:
- panels: bfloat16 [512, 64, 512], P(('groups', 'dec')), parts along dimension 0, may hold values from -6 to 6
- tile_panels: int32 [128, 16], P(('groups', 'dec')), parts along dimension 0, may hold values from 0 to 255, as said below
- tile_count: int32 [32], P(('groups', 'dec')), parts along dimension 0, may hold values from 1 to 4, as said below
- conv_weight: bfloat16 [3, 3, 3, 512, 256], replicated, may hold values from -0.0546875 to 0.0546875
- conv_bias: float32 [256], replicated, may hold values from -4 to 4
- norm_gain: float32 [256], replicated, may hold values from 0.1 to 1.9
- norm_shift: float32 [256], replicated, may hold values from -3 to 3
Outputs:
- decoded: bfloat16 [128, 392, 256], P(('groups', 'dec')), parts along dimension 0
There are 2 independent parts, one for each index of `groups`. A program takes and returns all parts, laid end to end along the dimension named above; an argument that names none is the same for every part. Nothing has to cross between parts.
Inputs may be any that keep to these rules, and one draw needn't show every extreme that they name: `tile_panels`: panel p lies on device p // 16. Over all 4 rows of one device, at most 4 entries name panels of any one device, repeats counted; in every draw each device's rows name exactly 4 panels on each of 16 devices. `tile_count`: in every draw some device has 4 live rows.
All inputs are finite; a program needn't handle non-finite values.
Results may differ from a plain program's by a relative error of at most 0.001.
Values may be sent and summed in bfloat16 or wider, within the bound.
No kernel may reach another device: no remote copies, remote signals or barrier semaphores. Data moves between devices by JAX's collectives and lax.ppermute only.
A program may use at most 128 MiB of HBM per device.

v0:
```python
import jax
import jax.numpy as jnp
from jax import lax
from jax.sharding import PartitionSpec as P

C_OUT = 256
GROUPS = 32
PH = 8
PW = 8
GH = 2
GW = 2
WT = 4
OCELLS = 392


epsilon = 1e-06


def arrange_window(panel_rows, frame_count, grid_high, grid_wide, panel_high, panel_wide):
    channels = panel_rows.shape[-1]
    blocks = panel_rows.reshape(frame_count, grid_high, grid_wide, panel_high, panel_wide, channels)
    blocks = blocks.transpose(0, 1, 3, 2, 4, 5)
    return blocks.reshape(frame_count, grid_high * panel_high, grid_wide * panel_wide, channels)


def decode_window(window, kernel, conv_bias, norm_gain, norm_shift, groups):
    out_frames = window.shape[0] - 2
    out_high = window.shape[1] - 2
    out_wide = window.shape[2] - 2
    pieces = []
    for tap_t in range(3):
        for tap_h in range(3):
            for tap_w in range(3):
                pieces.append(
                    window[
                        tap_t : tap_t + out_frames,
                        tap_h : tap_h + out_high,
                        tap_w : tap_w + out_wide,
                        :,
                    ]
                )
    columns = jnp.concatenate(pieces, axis=-1)
    columns = columns.reshape(out_frames * out_high * out_wide, columns.shape[-1])
    conv_out = jnp.dot(columns, kernel, preferred_element_type=jnp.float32) + conv_bias
    cell_count = conv_out.shape[0]
    width_out = conv_out.shape[1]
    grouped = conv_out.reshape(cell_count, groups, width_out // groups)
    center = jnp.mean(grouped, axis=(0, 2), keepdims=True)
    shifted = grouped - center
    spread = jnp.mean(shifted * shifted, axis=(0, 2), keepdims=True)
    normed = (shifted / jnp.sqrt(spread + epsilon)).reshape(cell_count, width_out)
    scaled = normed * norm_gain + norm_shift
    return jax.nn.silu(scaled).astype(jnp.bfloat16)


def fetch_panels(panels, work_rows, live_tiles, capacity):
    devices = lax.axis_size("dec")
    per_device = panels.shape[0]
    tile_rows, slot_count = work_rows.shape
    wanted = work_rows.reshape(tile_rows * slot_count)
    ref_live = jnp.arange(tile_rows * slot_count, dtype=jnp.int32) // slot_count < live_tiles
    owner_dev = wanted // per_device
    local_row = wanted % per_device
    device_ids = jnp.arange(devices, dtype=jnp.int32)
    matches = ((owner_dev[:, None] == device_ids[None, :]) & ref_live[:, None]).astype(jnp.int32)
    before = jnp.cumsum(matches, axis=0) - matches
    slot_rank = jnp.sum(before * matches, axis=1)
    where_to = owner_dev * capacity + slot_rank
    target = jnp.where(ref_live, where_to, devices * capacity)
    request = jnp.full((devices * capacity,), -1, jnp.int32).at[target].set(local_row, mode="drop")
    asked_rows = lax.all_to_all(
        request.reshape(devices, capacity), "dec", split_axis=0, concat_axis=0, tiled=True
    )
    picked = panels[jnp.maximum(asked_rows, 0)]
    returned = lax.all_to_all(picked, "dec", split_axis=0, concat_axis=0, tiled=True)
    landed = returned.reshape(devices * capacity, panels.shape[1], panels.shape[2])
    chosen = landed[jnp.where(ref_live, where_to, 0)]
    return chosen.reshape(tile_rows, slot_count, panels.shape[1], panels.shape[2])


def body(panels, tile_panels, tile_count, conv_weight, conv_bias, norm_gain, norm_shift):
    devices = lax.axis_size("dec")
    tile_rows, slot_count = tile_panels.shape
    capacity = max(1, tile_rows * slot_count // devices)
    kernel = conv_weight.reshape(27 * conv_weight.shape[3], conv_weight.shape[4])
    own_count = tile_count[0]
    windows = fetch_panels(panels, tile_panels, own_count, capacity)

    def decode_into(work, buffer, source_row, dest_row):
        window = arrange_window(work[source_row], WT, GH, GW, PH, PW)
        tile_out = decode_window(window, kernel, conv_bias, norm_gain, norm_shift, GROUPS)
        return lax.dynamic_update_slice_in_dim(buffer, tile_out[None], dest_row, 0)

    results = jnp.zeros((tile_rows, OCELLS, C_OUT), jnp.bfloat16)
    decoded = lax.fori_loop(
        0, own_count, lambda step, buffer: decode_into(windows, buffer, step, step), results
    )
    return decoded


def solution(mesh):
    in_specs = (
        P(("groups", "dec"), None, None),
        P(("groups", "dec"), None),
        P(("groups", "dec")),
        P(),
        P(),
        P(),
        P(),
    )
    out_specs = P(("groups", "dec"), None, None)
    return jax.shard_map(body, mesh=mesh, in_specs=in_specs, out_specs=out_specs, check_vma=False)
```

profile of v0, /device:TPU:15, one launch (start us, length us, event | category | flops | bytes accessed | tf_op | source)
XLA Modules:
  0.0 317.0 jit_solution(12587733459709594561)
XLA Ops:
  3.6 10.2 %all_to_all.14 = s32[16,1,4]{2,1,0:T(1,128)S(1)} all-to-all(s32[16,1,4]{2,1,0:T(1,128)S(1)} %bitcast.65), channel_id=1, replica_groups=mesh['groups'=2,'dec'=16] {'dec'}, dimensions={0} | all-to-all | bytes 512 | tf_op jit(solution)/shard_map/all_to_all | solution.py:71
  13.9 2.7 gather_fusion
  16.7 7.0 %all-to-all-start.1 = ((bf16[16,4,64,512]{3,2,1,0:T(8,128)(2,1)}), bf16[16,4,64,512]{3,2,1,0:T(8,128)(2,1)}, u32[]{:S(2)}, u32[]{:S(2)}) async-start(bf16[16,4,64,512]{3,2,1,0:T(8,128)(2,1)} %bitcast.64), calls=%async_computation.1 | async-start | bytes 8388608 | tf_op jit(solution)/shard_map/all_to_all | solution.py:75
  23.6 92.5 %all-to-all-done.1 = bf16[16,4,64,512]{3,2,1,0:T(8,128)(2,1)} async-done(((bf16[16,4,64,512]{3,2,1,0:T(8,128)(2,1)}), bf16[16,4,64,512]{3,2,1,0:T(8,128)(2,1)}, u32[]{:S(2)}, u32[]{:S(2)}) %all-to-all-start.1) | async-done | bytes 4194336 | tf_op jit(solution)/shard_map/all_to_all | solution.py:75
  116.1 4.9 %gather_fusion.1 = bf16[64,64,512]{2,1,0:T(8,128)(2,1)} fusion(bf16[64,64,512]{2,1,0:T(8,128)(2,1)} %bitcast.9, s32[1024]{0:T(1024)S(1)} %pad_clamp_fusion), kind=kCustom, calls=%fused_computation.1 | custom fusion | bytes 8388864 | tf_op jit(solution)/shard_map/gather | solution.py:77
  121.1 195.0 %while.10 = (s32[]{:T(128)}, bf16[4,392,256]{2,1,0:T(8,128)(2,1)S(1)}, s32[]{:T(128)}, bf16[4,16,64,512]{3,2,1,0:T(8,128)(2,1)}, bf16[13824,256]{1,0:T(8,128)(2,...) while((s32[]{:T(128)}, ...), condition=%wide.region_8.9_spmd, body=%wide.region_3.8_spmd.sunk | while | flops 2775937024 | bytes 68437160 | solution.py:95
  121.8 1.3 constant_dynamic-slice_fusion.2
  138.6 1.0 slice_dynamic-update-slice_fusion.71
  141.4 1.0 slice_dynamic-update-slice_fusion.74
  147.8 12.5 %reshape.269 = bf16[392,13824]{1,0:T(8,128)(2,1)} reshape(bf16[2,14,14,13824]{3,2,1,0:T(8,128)(2,1)} %slice_dynamic-update-slice_fusion.80) | data formatting | bytes 21676032 | tf_op jit(solution)/shard_map/while/body/reshape | solution.py:43
  160.3 8.4 %fusion.15 = (f32[256]{0:T(256)S(1)}, f32[392,256]{1,0:T(8,128)S(1)}) fusion(f32[256]{0:T(256)S(1)} %get-tuple-element.154, bf16[392,13824]{1,0:T(8,128)(2,1)} %reshape.269, bf16[13824,256]{1,0:T(8,128)(2,1)} %get-tuple-element.153), kind=kOutput, calls=%fused_computation.71.clone.1 | convolution fusion | flops 2774732544 | bytes 18319360 | tf_op jit(solution)/shard_map/while/body/dot_general | solution.py:44
  170.4 1.3 constant_dynamic-slice_fusion.2
  187.2 1.0 slice_dynamic-update-slice_fusion.71
  190.0 1.0 slice_dynamic-update-slice_fusion.74
  196.4 12.5 %reshape.269 = bf16[392,13824]{1,0:T(8,128)(2,1)} reshape(bf16[2,14,14,13824]{3,2,1,0:T(8,128)(2,1)} %slice_dynamic-update-slice_fusion.80) | data formatting | bytes 21676032 | tf_op jit(solution)/shard_map/while/body/reshape | solution.py:43
  208.9 8.4 %fusion.15 = (f32[256]{0:T(256)S(1)}, f32[392,256]{1,0:T(8,128)S(1)}) fusion(f32[256]{0:T(256)S(1)} %get-tuple-element.154, bf16[392,13824]{1,0:T(8,128)(2,1)} %reshape.269, bf16[13824,256]{1,0:T(8,128)(2,1)} %get-tuple-element.153), kind=kOutput, calls=%fused_computation.71.clone.1 | convolution fusion | flops 2774732544 | bytes 18319360 | tf_op jit(solution)/shard_map/while/body/dot_general | solution.py:44
  219.0 1.3 constant_dynamic-slice_fusion.2
  235.8 1.0 slice_dynamic-update-slice_fusion.71
  245.0 12.5 %reshape.269 = bf16[392,13824]{1,0:T(8,128)(2,1)} reshape(bf16[2,14,14,13824]{3,2,1,0:T(8,128)(2,1)} %slice_dynamic-update-slice_fusion.80) | data formatting | bytes 21676032 | tf_op jit(solution)/shard_map/while/body/reshape | solution.py:43
  257.5 8.4 %fusion.15 = (f32[256]{0:T(256)S(1)}, f32[392,256]{1,0:T(8,128)S(1)}) fusion(f32[256]{0:T(256)S(1)} %get-tuple-element.154, bf16[392,13824]{1,0:T(8,128)(2,1)} %reshape.269, bf16[13824,256]{1,0:T(8,128)(2,1)} %get-tuple-element.153), kind=kOutput, calls=%fused_computation.71.clone.1 | convolution fusion | flops 2774732544 | bytes 18319360 | tf_op jit(solution)/shard_map/while/body/dot_general | solution.py:44
  267.6 1.3 constant_dynamic-slice_fusion.2
  284.4 1.0 slice_dynamic-update-slice_fusion.71
  293.6 12.5 %reshape.269 = bf16[392,13824]{1,0:T(8,128)(2,1)} reshape(bf16[2,14,14,13824]{3,2,1,0:T(8,128)(2,1)} %slice_dynamic-update-slice_fusion.80) | data formatting | bytes 21676032 | tf_op jit(solution)/shard_map/while/body/reshape | solution.py:43
  306.1 8.4 %fusion.15 = (f32[256]{0:T(256)S(1)}, f32[392,256]{1,0:T(8,128)S(1)}) fusion(f32[256]{0:T(256)S(1)} %get-tuple-element.154, bf16[392,13824]{1,0:T(8,128)(2,1)} %reshape.269, bf16[13824,256]{1,0:T(8,128)(2,1)} %get-tuple-element.153), kind=kOutput, calls=%fused_computation.71.clone.1 | convolution fusion | flops 2774732544 | bytes 18319360 | tf_op jit(solution)/shard_map/while/body/dot_general | solution.py:44
  (180 shorter events, 100.7 us)
Async XLA Ops:
  0.0 13.9 %copy-start = (bf16[16,64,512]{2,1,0:T(8,128)(2,1)S(1)}, bf16[16,64,512]{2,1,0:T(8,128)(2,1)}, u32[]{:S(2)}) copy-start(bf16[16,64,512]{2,1,0:T(8,128)(2,1)} %param.9) | copy-start | bytes 3145732
  13.9 107.2 %copy-start.2 = (f32[256]{0:T(256)S(1)}, f32[256]{0:T(256)}, u32[]{:S(2)}) copy-start(f32[256]{0:T(256)} %param.14) | copy-start | bytes 3076
  13.9 107.2 %copy-start.3 = (f32[256]{0:T(256)S(1)}, f32[256]{0:T(256)}, u32[]{:S(2)}) copy-start(f32[256]{0:T(256)} %param.15) | copy-start | bytes 3076
  13.9 107.2 %copy-start.4 = (f32[256]{0:T(256)S(1)}, f32[256]{0:T(256)}, u32[]{:S(2)}) copy-start(f32[256]{0:T(256)} %param.13) | copy-start | bytes 3076
  16.7 99.4 %all-to-all-start.1 = ((bf16[16,4,64,512]{3,2,1,0:T(8,128)(2,1)}), bf16[16,4,64,512]{3,2,1,0:T(8,128)(2,1)}, u32[]{:S(2)}, u32[]{:S(2)}) async-start(bf16[16,4,64,512]{3,2,1,0:T(8,128)(2,1)} %bitcast.64), calls=%async_computation.1 | async-start | bytes 8388608 | tf_op jit(solution)/shard_map/all_to_all | solution.py:75
  316.1 0.9 copy-start.1
where the time goes:
time: 318 us; the launch traced here: 317 us
  local copies, waits for them, and re-layouts  167 us (53%)
  waiting for transfers between devices  92.5 us (29%)
  matrix products  33.5 us (11%)
  blocking collectives  10.2 us (3%)
  starting transfers between devices  6.96 us (2%)
  loops' own time  3.6 us (1%)
    while x104, local copies, waits for them, and re-layouts  94.6 us
    all_to_all x1, waiting for transfers between devices, fetch_panels(): lax.all_to_all(picked, 'dec', split_axis=0, concat_axis=0, tiled=True)  92.5 us
    reshape x4, local copies, waits for them, and re-layouts, decode_window(): columns.reshape(out_frames * out_high * out_wide, columns.shape[-1])  50 us
    dot_general x4, matrix products, decode_window(): jnp.dot(columns, kernel, preferred_element_type=jnp.float32) + conv_bias  33.5 us
    all_to_all x1, blocking collectives, fetch_panels(): lax.all_to_all(request.reshape(devices, capacity), 'dec', split_axis=0, c...  10.2 us
    all_to_all x1, starting transfers between devices, fetch_panels(): lax.all_to_all(picked, 'dec', split_axis=0, concat_axis=0, tiled=True)  6.96 us
  transfers between devices with their start and end apart: 1, of which 1 were waited for; matrix products, arithmetic and copies ran while one was open for 0% of the time, Pallas kernels for 0%

commit v1 on v0

v1 whole, which is shorter than its diff:
```python
import functools

import jax
import jax.numpy as jnp
import numpy as np
from jax import lax
from jax.experimental import pallas as pl
from jax.experimental.pallas import tpu as pltpu
from jax.sharding import PartitionSpec as P


C_OUT = 256
GROUPS = 32
PH = 8
PW = 8
GH = 2
GW = 2
WT = 4
OF = WT - 2
OH = GH * PH - 2
OW = GW * PW - 2
WIDE = GW * PW
OCELLS = OF * OH * OW
ROWS = OF * OH * WIDE
SPLIT = (256, 256)

epsilon = 1e-06


def requests(tile_panels, live_tiles, per_device, devices, capacity):
    tile_rows, slot_count = tile_panels.shape
    refs = tile_rows * slot_count
    wanted = tile_panels.reshape(refs)
    spot = jnp.arange(refs, dtype=jnp.int32)
    live = spot // slot_count < live_tiles
    owner = jnp.where(live, wanted // per_device, devices)
    local_row = wanted % per_device
    earlier = (owner[None, :] == owner[:, None]) & (spot[None, :] < spot[:, None])
    rank = jnp.sum(earlier.astype(jnp.int32), axis=1)
    where_to = owner * capacity + rank
    places = jnp.arange(devices * capacity, dtype=jnp.int32)
    hit = places[:, None] == where_to[None, :]
    packed = jnp.sum(jnp.where(hit, ((spot + 1) * per_device + local_row)[None, :], 0), axis=1)
    return packed % per_device, packed // per_device - 1


def pick_kernel(half, capacity, which, first, width, place, rows, source, *refs):
    outs, sem = refs[:-1], refs[-1]
    for begin in (True, False):
        for r in range(1, half):
            q = place[1] ^ r
            for k in range(capacity):
                row = rows[(q * 2 + which) * capacity + k]
                copy = pltpu.make_async_copy(
                    source.at[row, :, pl.ds(first, width)], outs[r - 1].at[k], sem.at[r - 1]
                )
                if begin:
                    copy.start()
                else:
                    copy.wait()


def pick(place, rows, source, half, capacity, which, first, width):
    cells = source.shape[1]
    smem = pl.BlockSpec(memory_space=pltpu.SMEM)
    shape = jax.ShapeDtypeStruct((capacity, cells, width), jnp.bfloat16)
    return pl.pallas_call(
        functools.partial(pick_kernel, half, capacity, which, first, width),
        out_shape=[shape] * (half - 1),
        in_specs=[smem, smem, pl.BlockSpec(memory_space=pl.ANY)],
        out_specs=[pl.BlockSpec(memory_space=pltpu.VMEM)] * (half - 1),
        scratch_shapes=[pltpu.SemaphoreType.DMA((half - 1,))],
        compiler_params=pltpu.CompilerParams(vmem_limit_bytes=8 * 2**20),
        cost_estimate=pl.CostEstimate(flops=0, bytes_accessed=4 * 2**20, transcendentals=0),
        name="pick",
    )(place, rows, source)


def conv_tile(window, weights, tile, first, width, between=()):
    sums = [None] * 3
    between = list(between)
    for a in range(3):
        for b in range(3):
            if between:
                between.pop(0)()
            cells = window[tile, a : a + OF, b : b + OH, :, :].reshape(ROWS, width)
            for c in range(3):
                part = jnp.dot(
                    cells,
                    weights[a, b, c, first : first + width],
                    preferred_element_type=jnp.float32,
                )
                sums[c] = part if sums[c] is None else sums[c] + part
    return sums[0] + pltpu.roll(sums[1], ROWS - 1, 0) + pltpu.roll(sums[2], ROWS - 2, 0)


def spread_groups(row):
    lane = lax.broadcasted_iota(jnp.int32, row.shape, 1)
    step = 1
    while step < C_OUT // GROUPS:
        low = (lane // step) % 2 == 0
        row = row + jnp.where(low, pltpu.roll(row, C_OUT - step, 1), pltpu.roll(row, step, 1))
        step *= 2
    return row


def finish_steps(load, take, bias, gain, shift, put):
    count = OCELLS * (C_OUT // GROUPS)
    held = {}

    def total(values):
        column = lax.broadcasted_iota(jnp.int32, (WIDE, C_OUT), 0)
        strip = jnp.where(column < OW, jnp.sum(values, axis=0), 0.0)
        return jnp.sum(strip, axis=0, keepdims=True)

    def strips():
        return load().reshape(OF * OH, WIDE, C_OUT)

    def first():
        held["sum"] = total(strips()) + bias * OCELLS

    def second():
        held["offset"] = bias - spread_groups(held["sum"]) / count

    def third():
        centred = strips() + held["offset"]
        held["square"] = total(centred * centred)

    def fourth():
        var = spread_groups(held["square"]) / count
        held["scale"] = gain / jnp.sqrt(var + epsilon)
        held["base"] = held["offset"] * held["scale"] + shift

    def fifth():
        scaled = load() * held["scale"] + held["base"]
        held["result"] = (scaled / (1.0 + jnp.exp(-scaled))).astype(jnp.bfloat16)

    def sixth():
        picked = jnp.dot(take, held["result"], preferred_element_type=jnp.float32)
        put(picked.astype(jnp.bfloat16))

    return [first, second, third, fourth, fifth, sixth]


def taken_cells():
    cell = np.arange(OCELLS)
    take = np.zeros((OCELLS, ROWS), np.float32)
    take[cell, cell // OW * WIDE + cell % OW] = 1.0
    return jnp.asarray(take, jnp.bfloat16)


def conv_kernel(plan, first, width, is_first, is_last, *refs):
    half, capacity, paired, counts = plan
    live_ref, place, asked, fills, weights = refs[:5]
    refs = refs[5:]
    groups = []
    for count in counts:
        groups.append(refs[:count])
        refs = refs[count:]
    if not is_first:
        partial, refs = refs[0], refs[1:]
    if is_last:
        take, bias, gain, shift = refs[:4]
        refs = refs[4:]
    out, window, result, sem, out_sem = refs[:5]
    rest = refs[5:]
    if not is_first:
        (before, before_sem), rest = rest[:2], rest[2:]
    if is_last:
        sums, blank, blank_sem = rest
    live = live_ref[0]
    slot_count = WT * GH * GW

    def bring(source, tile, slot):
        f, g, h = slot // (GH * GW), slot // GW % GH, slot % GW
        rows = pl.ds(pl.multiple_of(g * PH, PH), PH)
        columns = pl.ds(pl.multiple_of(h * PW, PW), PW)
        return pltpu.make_async_copy(source, window.at[tile, f, rows, columns, :], sem.at[tile])

    def fetch(tile):
        return pltpu.make_async_copy(partial.at[tile], before.at[tile], before_sem.at[tile])

    def store(tile):
        return pltpu.make_async_copy(result.at[tile], out.at[tile], out_sem.at[tile])

    def clear(tile):
        return pltpu.make_async_copy(blank, out.at[tile], blank_sem)

    for side in range(2):
        side_half = place[0] ^ side
        for r in range(half):
            q = place[1] ^ r if paired else r
            for k in range(capacity):
                at = (side_half * half + q) * capacity + k
                spot = fills[at]
                if not paired:
                    source = groups[side][0].at[r * capacity + k]
                elif r == 0:
                    begin = first if side == 0 else 0
                    source = groups[side][0].at[asked[at], :, :, pl.ds(begin, width)]
                else:
                    source = groups[side][r].at[k]

                @pl.when(spot >= 0)
                def _():
                    bring(source, spot // slot_count, spot % slot_count).start()

    if not is_first:

        def prefetch(tile, carry):
            fetch(tile).start()
            return carry

        lax.fori_loop(0, live, prefetch, 0)

    if is_last:
        blank[...] = jnp.zeros((OCELLS, C_OUT), jnp.bfloat16)

        def erase(tile, carry):
            clear(tile).start()
            return carry

        lax.fori_loop(live, result.shape[0], erase, 0)

    def arrive(tile):
        for _ in range(slot_count):
            bring(window.at[tile, 0, pl.ds(0, PH), pl.ds(0, PW), :], tile, 0).wait()
        if not is_first:
            fetch(tile).wait()

    def convolve(tile, between=()):
        conv = conv_tile(window, weights, tile, first, width, between)
        if not is_first:
            conv = conv + before[tile]
        if is_last:
            sums[tile % 2] = conv
        else:
            result[tile] = conv

    def finish(tile):
        if not is_last:
            return []

        def put(values):
            result[tile] = values

        return finish_steps(
            lambda: sums[tile % 2], take[...], bias[...], gain[...], shift[...], put
        )

    arrive(0)
    convolve(0)

    def decode(tile, carry):
        arrive(tile)
        convolve(tile, finish(tile - 1))
        store(tile - 1).start()
        return carry

    lax.fori_loop(1, live, decode, 0)
    for step in finish(live - 1):
        step()
    store(live - 1).start()

    def drain(tile, carry):
        store(tile).wait()
        return carry

    lax.fori_loop(0, live, drain, 0)
    if is_last:

        def drain_blank(tile, carry):
            clear(tile).wait()
            return carry

        lax.fori_loop(live, result.shape[0], drain_blank, 0)


def conv_step(plan, first, width, scalars, weights, arrays, partial, tail, tile_rows):
    smem = pl.BlockSpec(memory_space=pltpu.SMEM)
    hbm = pl.BlockSpec(memory_space=pl.ANY)
    vmem = pl.BlockSpec(memory_space=pltpu.VMEM)
    is_first, is_last = partial is None, tail is not None
    args = [*scalars, weights, *arrays]
    specs = [smem] * len(scalars) + [vmem] + [hbm] * len(arrays)
    sums = (tile_rows, ROWS, C_OUT)
    if is_last:
        result, kind = (tile_rows, OCELLS, C_OUT), jnp.bfloat16
    else:
        result, kind = sums, jnp.float32
    scratch = [
        pltpu.VMEM((tile_rows, WT, GH * PH, WIDE, width), jnp.bfloat16),
        pltpu.VMEM(result, kind),
        pltpu.SemaphoreType.DMA((tile_rows,)),
        pltpu.SemaphoreType.DMA((tile_rows,)),
    ]
    if not is_first:
        args.append(partial)
        specs.append(hbm)
        scratch += [pltpu.VMEM(sums, jnp.float32), pltpu.SemaphoreType.DMA((tile_rows,))]
    if is_last:
        args.extend(tail)
        specs.extend([vmem] * len(tail))
        scratch += [
            pltpu.VMEM((2, ROWS, C_OUT), jnp.float32),
            pltpu.VMEM((OCELLS, C_OUT), jnp.bfloat16),
            pltpu.SemaphoreType.DMA,
        ]
    flops = tile_rows * 2 * ROWS * 27 * width * C_OUT
    return pl.pallas_call(
        functools.partial(conv_kernel, plan, first, width, is_first, is_last),
        out_shape=jax.ShapeDtypeStruct(result, kind),
        in_specs=specs,
        out_specs=hbm,
        scratch_shapes=scratch,
        compiler_params=pltpu.CompilerParams(vmem_limit_bytes=24 * 2**20),
        cost_estimate=pl.CostEstimate(flops=flops, bytes_accessed=8 * 2**20, transcendentals=0),
        name="conv_last" if is_last else "conv_part",
    )(*args)


def decode_tiles(panels, tile_panels, tile_count, conv_weight, conv_bias, norm_gain, norm_shift):
    devices = lax.axis_size("dec")
    tile_rows, slot_count = tile_panels.shape
    per_device, cells, _ = panels.shape
    capacity = max(1, tile_rows * slot_count // devices)
    half = devices // 2
    paired = half <= 8 and half & (half - 1) == 0
    index = lax.axis_index("dec")
    mine, seat = index // half, index % half
    halves = [list(range(half)), list(range(half, devices))]
    swap = [(device, (device + half) % devices) for device in range(devices)]

    asked, fills = requests(tile_panels, tile_count[0], per_device, devices, capacity)
    by_half = asked.reshape(2, half, capacity)
    own_ask = lax.dynamic_index_in_dim(by_half, mine, 0, False)
    far_ask = lax.dynamic_index_in_dim(by_half, 1 - mine, 0, False)
    sent = jnp.stack([own_ask, far_ask], axis=1)
    got = lax.all_to_all(sent, "dec", 0, 0, tiled=True, axis_index_groups=halves)

    firsts = [sum(SPLIT[:n]) for n in range(len(SPLIT))]
    far = []
    source = panels
    for first, width in zip(firsts, SPLIT):
        if far:
            source, far[-1] = lax.optimization_barrier((panels, far[-1]))
        far.append(lax.ppermute(source[:, :, first : first + width], "dec", swap))

    rows = got.reshape(-1)
    place = jnp.stack([mine, seat])

    def exchange(source, which, first, width):
        if not paired:
            picked = source[got[:, which].reshape(-1), :, first : first + width]
            picked = picked.reshape(half, capacity, cells, width)
            landed = lax.all_to_all(picked, "dec", 0, 0, tiled=True, axis_index_groups=halves)
            return [landed.reshape(-1, PH, PW, width)]
        picked = pick(place, rows, source, half, capacity, which, first, width)
        landed = [source.reshape(-1, PH, PW, source.shape[2])]
        for r in range(1, half):
            pairs = [(d, d // half * half + (d % half ^ r)) for d in range(devices)]
            moved = lax.ppermute(picked[r - 1], "dec", pairs)
            landed.append(moved.reshape(capacity, PH, PW, width))
        return landed

    tail = [taken_cells(), *(v.reshape(1, C_OUT) for v in (conv_bias, norm_gain, norm_shift))]
    scalars = (tile_count, place, asked, fills)
    own = []
    for first, width in zip(firsts, SPLIT):
        own.append(exchange(panels, 0, first, width))
    partial = None
    for n, (first, width) in enumerate(zip(firsts, SPLIT)):
        brought = exchange(far[n], 1, 0, width)
        plan = (half, capacity, paired, (len(own[n]), len(brought)))
        partial = conv_step(
            plan, first, width, scalars, conv_weight, [*own[n], *brought], partial,
            tail if n == len(SPLIT) - 1 else None, tile_rows,
        )
    return partial


def solution(mesh):
    in_specs = (
        P(("groups", "dec"), None, None),
        P(("groups", "dec"), None),
        P(("groups", "dec")),
        P(),
        P(),
        P(),
        P(),
    )
    out_specs = P(("groups", "dec"), None, None)
    return jax.shard_map(decode_tiles, mesh=mesh, in_specs=in_specs, out_specs=out_specs, check_vma=False)
```

time: 318 us -> 120 us (0.38)
  the two profiles are of different devices: /device:TPU:15 before, /device:TPU:21 now
where the time goes in v1:
time: 120 us; the launch traced here: 119 us
  starting transfers between devices  42.4 us (35%)
  waiting for transfers between devices  34.7 us (29%)
  Pallas kernels  29.9 us (25%)
  local copies, waits for them, and re-layouts  10.6 us (9%)
    ppermute x28, starting transfers between devices, exchange(): moved = lax.ppermute(picked[r - 1], 'dec', pairs)  34.4 us
    pallas_call x2, Pallas kernels, conv_step(): pl.pallas_call(functools.partial(conv_kernel, plan, first, width, is_firs...  24.2 us
    ppermute x28, waiting for transfers between devices, exchange(): moved = lax.ppermute(picked[r - 1], 'dec', pairs)  23 us
    all_to_all x1, waiting for transfers between devices, decode_tiles(): lax.all_to_all(sent, 'dec', 0, 0, tiled=True, axis_index_groups=halves)  7.27 us
    unnamed x16, local copies, waits for them, and re-layouts  6.69 us
    pallas_call x4, Pallas kernels, pick(): pl.pallas_call(functools.partial(pick_kernel, half, capacity, which, firs...  5.69 us
    all_to_all x1, starting transfers between devices, decode_tiles(): lax.all_to_all(sent, 'dec', 0, 0, tiled=True, axis_index_groups=halves)  4.73 us
    ppermute x2, waiting for transfers between devices, decode_tiles(): far.append(lax.ppermute(source[:, :, first:first + width], 'dec', swap))  4.36 us
  transfers between devices with their start and end apart: 31, of which 12 were waited for; matrix products, arithmetic and copies ran while one was open for 3% of the time, Pallas kernels for 14%

profile of v1, /device:TPU:21, one launch (start us, length us, event | category | flops | bytes accessed | tf_op | source)
XLA Modules:
  0.0 119.1 jit_solution(15621768277262959042)
XLA Ops:
  3.9 4.7 %all-to-all-start = ((s32[8,2,4]{2,1,0:T(2,128)}), s32[8,2,4]{2,1,0:T(2,128)S(1)}, u32[]{:S(2)}, u32[]{:S(2)}) async-start(s32[8,2,4]{2,1,0:T(2,128)} %copy.20), calls=%async_computation | async-start | bytes 16384 | tf_op jit(solution)/shard_map/all_to_all | solution.py:339
  8.7 7.3 %all-to-all-done = s32[8,2,4]{2,1,0:T(2,128)S(1)} async-done(((s32[8,2,4]{2,1,0:T(2,128)}), s32[8,2,4]{2,1,0:T(2,128)S(1)}, u32[]{:S(2)}, u32[]{:S(2)}) %all-to-all-start) | async-done | bytes 288 | tf_op jit(solution)/shard_map/all_to_all | solution.py:339
  18.7 4.4 %collective-permute-done.7.source = bf16[16,64,256]{2,1,0:T(8,128)(2,1)S(1)} collective-permute-done((bf16[16,64,256]{2,1,0:T(8,128)(2,1)S(1)}, bf16[16,64,256]{2,1,0:T(8,128)(2,1)S(1)}, u32[]{:S(2)}, u32[]{:S(2)}) %collective-permute-start.7) | collective-permute-done | bytes 524320 | tf_op jit(solution)/shard_map/ppermute | solution.py:347
  24.1 3.2 %collective-permute-start.8 = (bf16[16,64,256]{2,1,0:T(8,128)(2,1)S(1)}, bf16[16,64,256]{2,1,0:T(8,128)(2,1)S(1)}, u32[]{:S(2)}, u32[]{:S(2)}) collective-permute-start(bf16[16,64,256]{2,1,0:T(8,128)(2,1)S(1)} %slice.7), channel_id=1, source_target_pairs={{0,8},{1,9},{2,10},{3,11},{4,12},{5,13},{6,14},{7,15},{8,0},{9,1},... | collective-permute-start | bytes 1572872 | tf_op jit(solution)/shard_map/ppermute | solution.py:347
  28.5 2.2 %collective-permute-start.18 = (bf16[4,64,256]{2,1,0:T(8,128)(2,1)S(1)}, bf16[4,64,256]{2,1,0:T(8,128)(2,1)S(1)}, u32[]{:S(2)}, u32[]{:S(2)}) collective-permute-start(bf16[4,64,256]{2,1,0:T(8,128)(2,1)S(1)} %get-tuple-element.52), channel_id=1, source_target_pairs={{0,3},{1,2},{2,1},{3,0},{4,7},{5,6},{6,5},{7,4},{8,11},{9,10},{10,... | collective-permute-start | bytes 393224 | tf_op jit(solution)/shard_map/ppermute | solution.py:362
  34.4 1.8 %collective-permute-start.21 = (bf16[4,64,256]{2,1,0:T(8,128)(2,1)S(1)}, bf16[4,64,256]{2,1,0:T(8,128)(2,1)S(1)}, u32[]{:S(2)}, u32[]{:S(2)}) collective-permute-start(bf16[4,64,256]{2,1,0:T(8,128)(2,1)S(1)} %get-tuple-element.55), channel_id=1, source_target_pairs={{0,6},{1,7},{2,4},{3,5},{4,2},{5,3},{6,0},{7,1},{8,14},{9,15},{10,... | collective-permute-start | bytes 393224 | tf_op jit(solution)/shard_map/ppermute | solution.py:362
  36.5 1.6 %collective-permute-start.22 = (bf16[4,64,256]{2,1,0:T(8,128)(2,1)S(1)}, bf16[4,64,256]{2,1,0:T(8,128)(2,1)S(1)}, u32[]{:S(2)}, u32[]{:S(2)}) collective-permute-start(bf16[4,64,256]{2,1,0:T(8,128)(2,1)S(1)} %get-tuple-element.56), channel_id=1, source_target_pairs={{0,7},{1,6},{2,5},{3,4},{4,3},{5,2},{6,1},{7,0},{8,15},{9,14},{10,... | collective-permute-start | bytes 393224 | tf_op jit(solution)/shard_map/ppermute | solution.py:362
  38.1 6.0 %collective-permute-done.19 = bf16[4,64,256]{2,1,0:T(8,128)(2,1)S(1)} collective-permute-done((bf16[4,64,256]{2,1,0:T(8,128)(2,1)S(1)}, bf16[4,64,256]{2,1,0:T(8,128)(2,1)S(1)}, u32[]{:S(2)}, u32[]{:S(2)}) %collective-permute-start.19) | collective-permute-done | bytes 131104 | tf_op jit(solution)/shard_map/ppermute | solution.py:362
  45.0 3.0 %collective-permute-done.20 = bf16[4,64,256]{2,1,0:T(8,128)(2,1)S(1)} collective-permute-done((bf16[4,64,256]{2,1,0:T(8,128)(2,1)S(1)}, bf16[4,64,256]{2,1,0:T(8,128)(2,1)S(1)}, u32[]{:S(2)}, u32[]{:S(2)}) %collective-permute-start.20) | collective-permute-done | bytes 131104 | tf_op jit(solution)/shard_map/ppermute | solution.py:362
  48.1 3.3 %collective-permute-done.21 = bf16[4,64,256]{2,1,0:T(8,128)(2,1)S(1)} collective-permute-done((bf16[4,64,256]{2,1,0:T(8,128)(2,1)S(1)}, bf16[4,64,256]{2,1,0:T(8,128)(2,1)S(1)}, u32[]{:S(2)}, u32[]{:S(2)}) %collective-permute-start.21) | collective-permute-done | bytes 131104 | tf_op jit(solution)/shard_map/ppermute | solution.py:362
  51.4 4.0 %collective-permute-start.6 = (bf16[4,64,256]{2,1,0:T(8,128)(2,1)S(1)}, bf16[4,64,256]{2,1,0:T(8,128)(2,1)S(1)}, u32[]{:S(2)}, u32[]{:S(2)}) collective-permute-start(bf16[4,64,256]{2,1,0:T(8,128)(2,1)S(1)} %get-tuple-element.41), channel_id=1, source_target_pairs={{0,7},{1,6},{2,5},{3,4},{4,3},{5,2},{6,1},{7,0},{8,15},{9,14},{10,... | collective-permute-start | bytes 393224 | tf_op jit(solution)/shard_map/ppermute | solution.py:362
  55.4 1.6 %collective-permute-done.4 = bf16[4,64,256]{2,1,0:T(8,128)(2,1)S(1)} collective-permute-done((bf16[4,64,256]{2,1,0:T(8,128)(2,1)S(1)}, bf16[4,64,256]{2,1,0:T(8,128)(2,1)S(1)}, u32[]{:S(2)}, u32[]{:S(2)}) %collective-permute-start.4) | collective-permute-done | bytes 131104 | tf_op jit(solution)/shard_map/ppermute | solution.py:362
  59.8 2.0 %collective-permute-start.2 = (bf16[4,64,256]{2,1,0:T(8,128)(2,1)S(1)}, bf16[4,64,256]{2,1,0:T(8,128)(2,1)S(1)}, u32[]{:S(2)}, u32[]{:S(2)}) collective-permute-start(bf16[4,64,256]{2,1,0:T(8,128)(2,1)S(1)} %get-tuple-element.37), channel_id=1, source_target_pairs={{0,3},{1,2},{2,1},{3,0},{4,7},{5,6},{6,5},{7,4},{8,11},{9,10},{10,... | collective-permute-start | bytes 393224 | tf_op jit(solution)/shard_map/ppermute | solution.py:362
  61.8 1.9 %pick.7 = (bf16[4,64,256]{2,1,0:T(8,128)(2,1)S(1)}, bf16[4,64,256]{2,1,0:T(8,128)(2,1)S(1)}, bf16[4,64,256]{2,1,0:T(8,128)(2,1)S(1)}, bf16[4,64,256]{2,1,0:T(8,1...) custom-call(s32[2]{0:T(128)S(1)} %pad_add_fusion.1.place.refs_1_, ...), custom_call_target="tpu_custom_call" | custom-call | bytes 4194304 | tf_op jit(solution)/shard_map/pick/pallas_call | solution.py:67
  63.8 2.4 %collective-permute-start.3 = (bf16[4,64,256]{2,1,0:T(8,128)(2,1)S(1)}, bf16[4,64,256]{2,1,0:T(8,128)(2,1)S(1)}, u32[]{:S(2)}, u32[]{:S(2)}) collective-permute-start(bf16[4,64,256]{2,1,0:T(8,128)(2,1)S(1)} %get-tuple-element.38), channel_id=1, source_target_pairs={{0,4},{1,5},{2,6},{3,7},{4,0},{5,1},{6,2},{7,3},{8,12},{9,13},{10,... | collective-permute-start | bytes 393224 | tf_op jit(solution)/shard_map/ppermute | solution.py:362
  68.6 3.5 %collective-permute-start.26 = (bf16[4,64,256]{2,1,0:T(8,128)(2,1)S(1)}, bf16[4,64,256]{2,1,0:T(8,128)(2,1)S(1)}, u32[]{:S(2)}, u32[]{:S(2)}) collective-permute-start(bf16[4,64,256]{2,1,0:T(8,128)(2,1)S(1)} %get-tuple-element.61), channel_id=1, source_target_pairs={{0,4},{1,5},{2,6},{3,7},{4,0},{5,1},{6,2},{7,3},{8,12},{9,13},{10,... | collective-permute-start | bytes 393224 | tf_op jit(solution)/shard_map/ppermute | solution.py:362
  72.2 1.9 %pick.5 = (bf16[4,64,256]{2,1,0:T(8,128)(2,1)S(1)}, bf16[4,64,256]{2,1,0:T(8,128)(2,1)S(1)}, bf16[4,64,256]{2,1,0:T(8,128)(2,1)S(1)}, bf16[4,64,256]{2,1,0:T(8,1...) custom-call(s32[2]{0:T(128)S(1)} %pad_add_fusion.1.place.refs_1_, ...), custom_call_target="tpu_custom_call" | custom-call | bytes 4194304 | tf_op jit(solution)/shard_map/pick/pallas_call | solution.py:67
  74.3 2.6 %collective-permute-start.28 = (bf16[4,64,256]{2,1,0:T(8,128)(2,1)S(1)}, bf16[4,64,256]{2,1,0:T(8,128)(2,1)S(1)}, u32[]{:S(2)}, u32[]{:S(2)}) collective-permute-start(bf16[4,64,256]{2,1,0:T(8,128)(2,1)S(1)} %get-tuple-element.63), channel_id=1, source_target_pairs={{0,6},{1,7},{2,4},{3,5},{4,2},{5,3},{6,0},{7,1},{8,14},{9,15},{10,... | collective-permute-start | bytes 393224 | tf_op jit(solution)/shard_map/ppermute | solution.py:362
  81.3 2.3 %collective-permute-done.28 = bf16[4,64,256]{2,1,0:T(8,128)(2,1)S(1)} collective-permute-done((bf16[4,64,256]{2,1,0:T(8,128)(2,1)S(1)}, bf16[4,64,256]{2,1,0:T(8,128)(2,1)S(1)}, u32[]{:S(2)}, u32[]{:S(2)}) %collective-permute-start.28) | collective-permute-done | bytes 131104 | tf_op jit(solution)/shard_map/ppermute | solution.py:362
  83.7 2.9 %collective-permute-done.29 = bf16[4,64,256]{2,1,0:T(8,128)(2,1)S(1)} collective-permute-done((bf16[4,64,256]{2,1,0:T(8,128)(2,1)S(1)}, bf16[4,64,256]{2,1,0:T(8,128)(2,1)S(1)}, u32[]{:S(2)}, u32[]{:S(2)}) %collective-permute-start.29) | collective-permute-done | bytes 131104 | tf_op jit(solution)/shard_map/ppermute | solution.py:362
  88.3 2.0 %collective-permute-start.15 = (bf16[4,64,256]{2,1,0:T(8,128)(2,1)S(1)}, bf16[4,64,256]{2,1,0:T(8,128)(2,1)S(1)}, u32[]{:S(2)}, u32[]{:S(2)}) collective-permute-start(bf16[4,64,256]{2,1,0:T(8,128)(2,1)S(1)} %get-tuple-element.49), channel_id=1, source_target_pairs={{0,7},{1,6},{2,5},{3,4},{4,3},{5,2},{6,1},{7,0},{8,15},{9,14},{10,... | collective-permute-start | bytes 393224 | tf_op jit(solution)/shard_map/ppermute | solution.py:362
  91.6 3.0 %copy-done.3 = bf16[3,3,3,512,256]{4,3,2,1,0:T(8,128)(2,1)S(1)} copy-done((bf16[3,3,3,512,256]{4,3,2,1,0:T(8,128)(2,1)S(1)}, bf16[3,3,3,512,256]{4,3,2,1,0:T(8,128)(2,1)}, u32[]{:S(2)}) %copy-start.3) | copy-done | bytes 7077912
  94.6 11.0 %conv_part.1.refs_21_ = f32[4,448,256]{2,1,0:T(8,128)S(1)} custom-call(s32[1]{0:T(128)} %copy.21.refs_0_, s32[2]{0:T(128)S(1)} %pad_add_fusion.1.place.refs_1_, s32[64]{0:T(128)S(1)} %get-tuple-element.68.refs_2_, s32[64]{0:T(128)S(1)} %get-tuple-element.67.refs_3_, bf16[3,3,3,512,256]{4,3,2,1,0:T(8,128)(2,1)S(1)} %copy-done.3, ...), custom_call_target="tpu_custom_call" | custom-call | flops 6341787648 | bytes 8388608 | tf_op jit(solution)/shard_map/conv_part/pallas_call | solution.py:310
  105.7 13.2 %conv_last.1 = bf16[4,392,256]{2,1,0:T(8,128)(2,1)} custom-call(s32[1]{0:T(128)} %copy.21.refs_0_, s32[2]{0:T(128)S(1)} %pad_add_fusion.1.place.refs_1_, s32[64]{0:T(128)S(1)} %get-tuple-element.68.refs_2_, s32[64]{0:T(128)S(1)} %get-tuple-element.67.refs_3_, bf16[3,3,3,512,256]{4,3,2,1,0:T(8,128)(2,1)S(1)} %copy-done.3, ...), custom_call_target="tpu_custom_call" | custom-call | flops 6341787648 | bytes 8388608 | tf_op jit(solution)/shard_map/conv_last/pallas_call | solution.py:310
  (77 shorter events, 26.1 us)
Async XLA Ops:
  1.1 22.0 %collective-permute-start.7 = (bf16[16,64,256]{2,1,0:T(8,128)(2,1)S(1)}, bf16[16,64,256]{2,1,0:T(8,128)(2,1)S(1)}, u32[]{:S(2)}, u32[]{:S(2)}) collective-permute-start(bf16[16,64,256]{2,1,0:T(8,128)(2,1)S(1)} %slice.6), channel_id=1, source_target_pairs={{0,8},{1,9},{2,10},{3,11},{4,12},{5,13},{6,14},{7,15},{8,0},{9,1},... | collective-permute-start | bytes 1572872 | tf_op jit(solution)/shard_map/ppermute | solution.py:347
  3.9 12.1 %all-to-all-start = ((s32[8,2,4]{2,1,0:T(2,128)}), s32[8,2,4]{2,1,0:T(2,128)S(1)}, u32[]{:S(2)}, u32[]{:S(2)}) async-start(s32[8,2,4]{2,1,0:T(2,128)} %copy.20), calls=%async_computation | async-start | bytes 16384 | tf_op jit(solution)/shard_map/all_to_all | solution.py:339
  18.2 13.4 %collective-permute-start.16 = (bf16[4,64,256]{2,1,0:T(8,128)(2,1)S(1)}, bf16[4,64,256]{2,1,0:T(8,128)(2,1)S(1)}, u32[]{:S(2)}, u32[]{:S(2)}) collective-permute-start(bf16[4,64,256]{2,1,0:T(8,128)(2,1)S(1)} %get-tuple-element.50), channel_id=1, source_target_pairs={{0,1},{1,0},{2,3},{3,2},{4,5},{5,4},{6,7},{7,6},{8,9},{9,8},{10,11... | collective-permute-start | bytes 393224 | tf_op jit(solution)/shard_map/ppermute | solution.py:362
  24.1 44.5 %collective-permute-start.8 = (bf16[16,64,256]{2,1,0:T(8,128)(2,1)S(1)}, bf16[16,64,256]{2,1,0:T(8,128)(2,1)S(1)}, u32[]{:S(2)}, u32[]{:S(2)}) collective-permute-start(bf16[16,64,256]{2,1,0:T(8,128)(2,1)S(1)} %slice.7), channel_id=1, source_target_pairs={{0,8},{1,9},{2,10},{3,11},{4,12},{5,13},{6,14},{7,15},{8,0},{9,1},... | collective-permute-start | bytes 1572872 | tf_op jit(solution)/shard_map/ppermute | solution.py:347
  30.7 13.4 %collective-permute-start.19 = (bf16[4,64,256]{2,1,0:T(8,128)(2,1)S(1)}, bf16[4,64,256]{2,1,0:T(8,128)(2,1)S(1)}, u32[]{:S(2)}, u32[]{:S(2)}) collective-permute-start(bf16[4,64,256]{2,1,0:T(8,128)(2,1)S(1)} %get-tuple-element.53), channel_id=1, source_target_pairs={{0,4},{1,5},{2,6},{3,7},{4,0},{5,1},{6,2},{7,3},{8,12},{9,13},{10,... | collective-permute-start | bytes 393224 | tf_op jit(solution)/shard_map/ppermute | solution.py:362
  31.7 16.3 %collective-permute-start.20 = (bf16[4,64,256]{2,1,0:T(8,128)(2,1)S(1)}, bf16[4,64,256]{2,1,0:T(8,128)(2,1)S(1)}, u32[]{:S(2)}, u32[]{:S(2)}) collective-permute-start(bf16[4,64,256]{2,1,0:T(8,128)(2,1)S(1)} %get-tuple-element.54), channel_id=1, source_target_pairs={{0,5},{1,4},{2,7},{3,6},{4,1},{5,0},{6,3},{7,2},{8,13},{9,12},{10,... | collective-permute-start | bytes 393224 | tf_op jit(solution)/shard_map/ppermute | solution.py:362
  34.4 17.0 %collective-permute-start.21 = (bf16[4,64,256]{2,1,0:T(8,128)(2,1)S(1)}, bf16[4,64,256]{2,1,0:T(8,128)(2,1)S(1)}, u32[]{:S(2)}, u32[]{:S(2)}) collective-permute-start(bf16[4,64,256]{2,1,0:T(8,128)(2,1)S(1)} %get-tuple-element.55), channel_id=1, source_target_pairs={{0,6},{1,7},{2,4},{3,5},{4,2},{5,3},{6,0},{7,1},{8,14},{9,15},{10,... | collective-permute-start | bytes 393224 | tf_op jit(solution)/shard_map/ppermute | solution.py:362
  36.5 18.9 %collective-permute-start.22 = (bf16[4,64,256]{2,1,0:T(8,128)(2,1)S(1)}, bf16[4,64,256]{2,1,0:T(8,128)(2,1)S(1)}, u32[]{:S(2)}, u32[]{:S(2)}) collective-permute-start(bf16[4,64,256]{2,1,0:T(8,128)(2,1)S(1)} %get-tuple-element.56), channel_id=1, source_target_pairs={{0,7},{1,6},{2,5},{3,4},{4,3},{5,2},{6,1},{7,0},{8,15},{9,14},{10,... | collective-permute-start | bytes 393224 | tf_op jit(solution)/shard_map/ppermute | solution.py:362
  44.1 12.9 %collective-permute-start.4 = (bf16[4,64,256]{2,1,0:T(8,128)(2,1)S(1)}, bf16[4,64,256]{2,1,0:T(8,128)(2,1)S(1)}, u32[]{:S(2)}, u32[]{:S(2)}) collective-permute-start(bf16[4,64,256]{2,1,0:T(8,128)(2,1)S(1)} %get-tuple-element.39), channel_id=1, source_target_pairs={{0,5},{1,4},{2,7},{3,6},{4,1},{5,0},{6,3},{7,2},{8,13},{9,12},{10,... | collective-permute-start | bytes 393224 | tf_op jit(solution)/shard_map/ppermute | solution.py:362
  48.0 11.9 %collective-permute-start.5 = (bf16[4,64,256]{2,1,0:T(8,128)(2,1)S(1)}, bf16[4,64,256]{2,1,0:T(8,128)(2,1)S(1)}, u32[]{:S(2)}, u32[]{:S(2)}) collective-permute-start(bf16[4,64,256]{2,1,0:T(8,128)(2,1)S(1)} %get-tuple-element.40), channel_id=1, source_target_pairs={{0,6},{1,7},{2,4},{3,5},{4,2},{5,3},{6,0},{7,1},{8,14},{9,15},{10,... | collective-permute-start | bytes 393224 | tf_op jit(solution)/shard_map/ppermute | solution.py:362
  51.4 12.4 %collective-permute-start.6 = (bf16[4,64,256]{2,1,0:T(8,128)(2,1)S(1)}, bf16[4,64,256]{2,1,0:T(8,128)(2,1)S(1)}, u32[]{:S(2)}, u32[]{:S(2)}) collective-permute-start(bf16[4,64,256]{2,1,0:T(8,128)(2,1)S(1)} %get-tuple-element.41), channel_id=1, source_target_pairs={{0,7},{1,6},{2,5},{3,4},{4,3},{5,2},{6,1},{7,0},{8,15},{9,14},{10,... | collective-permute-start | bytes 393224 | tf_op jit(solution)/shard_map/ppermute | solution.py:362
  55.4 10.8 %collective-permute-start = (bf16[4,64,256]{2,1,0:T(8,128)(2,1)S(1)}, bf16[4,64,256]{2,1,0:T(8,128)(2,1)S(1)}, u32[]{:S(2)}, u32[]{:S(2)}) collective-permute-start(bf16[4,64,256]{2,1,0:T(8,128)(2,1)S(1)} %get-tuple-element.35), channel_id=1, source_target_pairs={{0,1},{1,0},{2,3},{3,2},{4,5},{5,4},{6,7},{7,6},{8,9},{9,8},{10,11... | collective-permute-start | bytes 393224 | tf_op jit(solution)/shard_map/ppermute | solution.py:362
  57.0 9.7 %collective-permute-start.1 = (bf16[4,64,256]{2,1,0:T(8,128)(2,1)S(1)}, bf16[4,64,256]{2,1,0:T(8,128)(2,1)S(1)}, u32[]{:S(2)}, u32[]{:S(2)}) collective-permute-start(bf16[4,64,256]{2,1,0:T(8,128)(2,1)S(1)} %get-tuple-element.36), channel_id=1, source_target_pairs={{0,2},{1,3},{2,0},{3,1},{4,6},{5,7},{6,4},{7,5},{8,10},{9,11},{10,... | collective-permute-start | bytes 393224 | tf_op jit(solution)/shard_map/ppermute | solution.py:362
  63.8 10.3 %collective-permute-start.3 = (bf16[4,64,256]{2,1,0:T(8,128)(2,1)S(1)}, bf16[4,64,256]{2,1,0:T(8,128)(2,1)S(1)}, u32[]{:S(2)}, u32[]{:S(2)}) collective-permute-start(bf16[4,64,256]{2,1,0:T(8,128)(2,1)S(1)} %get-tuple-element.38), channel_id=1, source_target_pairs={{0,4},{1,5},{2,6},{3,7},{4,0},{5,1},{6,2},{7,3},{8,12},{9,13},{10,... | collective-permute-start | bytes 393224 | tf_op jit(solution)/shard_map/ppermute | solution.py:362
  66.7 10.3 %collective-permute-start.24 = (bf16[4,64,256]{2,1,0:T(8,128)(2,1)S(1)}, bf16[4,64,256]{2,1,0:T(8,128)(2,1)S(1)}, u32[]{:S(2)}, u32[]{:S(2)}) collective-permute-start(bf16[4,64,256]{2,1,0:T(8,128)(2,1)S(1)} %get-tuple-element.59), channel_id=1, source_target_pairs={{0,2},{1,3},{2,0},{3,1},{4,6},{5,7},{6,4},{7,5},{8,10},{9,11},{10,... | collective-permute-start | bytes 393224 | tf_op jit(solution)/shard_map/ppermute | solution.py:362
  74.3 9.3 %collective-permute-start.28 = (bf16[4,64,256]{2,1,0:T(8,128)(2,1)S(1)}, bf16[4,64,256]{2,1,0:T(8,128)(2,1)S(1)}, u32[]{:S(2)}, u32[]{:S(2)}) collective-permute-start(bf16[4,64,256]{2,1,0:T(8,128)(2,1)S(1)} %get-tuple-element.63), channel_id=1, source_target_pairs={{0,6},{1,7},{2,4},{3,5},{4,2},{5,3},{6,0},{7,1},{8,14},{9,15},{10,... | collective-permute-start | bytes 393224 | tf_op jit(solution)/shard_map/ppermute | solution.py:362
  77.0 9.6 %collective-permute-start.29 = (bf16[4,64,256]{2,1,0:T(8,128)(2,1)S(1)}, bf16[4,64,256]{2,1,0:T(8,128)(2,1)S(1)}, u32[]{:S(2)}, u32[]{:S(2)}) collective-permute-start(bf16[4,64,256]{2,1,0:T(8,128)(2,1)S(1)} %get-tuple-element.64), channel_id=1, source_target_pairs={{0,7},{1,6},{2,5},{3,4},{4,3},{5,2},{6,1},{7,0},{8,15},{9,14},{10,... | collective-permute-start | bytes 393224 | tf_op jit(solution)/shard_map/ppermute | solution.py:362
  77.4 9.5 %collective-permute-start.9 = (bf16[4,64,256]{2,1,0:T(8,128)(2,1)S(1)}, bf16[4,64,256]{2,1,0:T(8,128)(2,1)S(1)}, u32[]{:S(2)}, u32[]{:S(2)}) collective-permute-start(bf16[4,64,256]{2,1,0:T(8,128)(2,1)S(1)} %get-tuple-element.43), channel_id=1, source_target_pairs={{0,1},{1,0},{2,3},{3,2},{4,5},{5,4},{6,7},{7,6},{8,9},{9,8},{10,11... | collective-permute-start | bytes 393224 | tf_op jit(solution)/shard_map/ppermute | solution.py:362
  77.4 10.9 %collective-permute-start.10 = (bf16[4,64,256]{2,1,0:T(8,128)(2,1)S(1)}, bf16[4,64,256]{2,1,0:T(8,128)(2,1)S(1)}, u32[]{:S(2)}, u32[]{:S(2)}) collective-permute-start(bf16[4,64,256]{2,1,0:T(8,128)(2,1)S(1)} %get-tuple-element.44), channel_id=1, source_target_pairs={{0,2},{1,3},{2,0},{3,1},{4,6},{5,7},{6,4},{7,5},{8,10},{9,11},{10,... | collective-permute-start | bytes 393224 | tf_op jit(solution)/shard_map/ppermute | solution.py:362
  80.0 25.6 %collective-permute-start.11 = (bf16[4,64,256]{2,1,0:T(8,128)(2,1)S(1)}, bf16[4,64,256]{2,1,0:T(8,128)(2,1)S(1)}, u32[]{:S(2)}, u32[]{:S(2)}) collective-permute-start(bf16[4,64,256]{2,1,0:T(8,128)(2,1)S(1)} %get-tuple-element.45), channel_id=1, source_target_pairs={{0,3},{1,2},{2,1},{3,0},{4,7},{5,6},{6,5},{7,4},{8,11},{9,10},{10,... | collective-permute-start | bytes 393224 | tf_op jit(solution)/shard_map/ppermute | solution.py:362
  83.6 22.0 %collective-permute-start.12 = (bf16[4,64,256]{2,1,0:T(8,128)(2,1)S(1)}, bf16[4,64,256]{2,1,0:T(8,128)(2,1)S(1)}, u32[]{:S(2)}, u32[]{:S(2)}) collective-permute-start(bf16[4,64,256]{2,1,0:T(8,128)(2,1)S(1)} %get-tuple-element.46), channel_id=1, source_target_pairs={{0,4},{1,5},{2,6},{3,7},{4,0},{5,1},{6,2},{7,3},{8,12},{9,13},{10,... | collective-permute-start | bytes 393224 | tf_op jit(solution)/shard_map/ppermute | solution.py:362
  86.6 19.0 %collective-permute-start.13 = (bf16[4,64,256]{2,1,0:T(8,128)(2,1)S(1)}, bf16[4,64,256]{2,1,0:T(8,128)(2,1)S(1)}, u32[]{:S(2)}, u32[]{:S(2)}) collective-permute-start(bf16[4,64,256]{2,1,0:T(8,128)(2,1)S(1)} %get-tuple-element.47), channel_id=1, source_target_pairs={{0,5},{1,4},{2,7},{3,6},{4,1},{5,0},{6,3},{7,2},{8,13},{9,12},{10,... | collective-permute-start | bytes 393224 | tf_op jit(solution)/shard_map/ppermute | solution.py:362
  86.8 18.8 %collective-permute-start.14 = (bf16[4,64,256]{2,1,0:T(8,128)(2,1)S(1)}, bf16[4,64,256]{2,1,0:T(8,128)(2,1)S(1)}, u32[]{:S(2)}, u32[]{:S(2)}) collective-permute-start(bf16[4,64,256]{2,1,0:T(8,128)(2,1)S(1)} %get-tuple-element.48), channel_id=1, source_target_pairs={{0,6},{1,7},{2,4},{3,5},{4,2},{5,3},{6,0},{7,1},{8,14},{9,15},{10,... | collective-permute-start | bytes 393224 | tf_op jit(solution)/shard_map/ppermute | solution.py:362
  88.3 17.3 %collective-permute-start.15 = (bf16[4,64,256]{2,1,0:T(8,128)(2,1)S(1)}, bf16[4,64,256]{2,1,0:T(8,128)(2,1)S(1)}, u32[]{:S(2)}, u32[]{:S(2)}) collective-permute-start(bf16[4,64,256]{2,1,0:T(8,128)(2,1)S(1)} %get-tuple-element.49), channel_id=1, source_target_pairs={{0,7},{1,6},{2,5},{3,4},{4,3},{5,2},{6,1},{7,0},{8,15},{9,14},{10,... | collective-permute-start | bytes 393224 | tf_op jit(solution)/shard_map/ppermute | solution.py:362
  (15 other events, 106.3 us)

commit v2 on v1

--- a/solution.py
+++ b/solution.py
@@ -47,12 +47,12 @@
 def pick_kernel(half, capacity, which, first, width, place, rows, source, *refs):
     outs, sem = refs[:-1], refs[-1]
     for begin in (True, False):
-        for r in range(1, half):
+        for r in range(half):
             q = place[1] ^ r
             for k in range(capacity):
                 row = rows[(q * 2 + which) * capacity + k]
                 copy = pltpu.make_async_copy(
-                    source.at[row, :, pl.ds(first, width)], outs[r - 1].at[k], sem.at[r - 1]
+                    source.at[row, :, pl.ds(first, width)], outs[r].at[k], sem.at[r]
                 )
                 if begin:
                     copy.start()
@@ -66,12 +66,12 @@
     shape = jax.ShapeDtypeStruct((capacity, cells, width), jnp.bfloat16)
     return pl.pallas_call(
         functools.partial(pick_kernel, half, capacity, which, first, width),
-        out_shape=[shape] * (half - 1),
+        out_shape=[shape] * half,
         in_specs=[smem, smem, pl.BlockSpec(memory_space=pl.ANY)],
-        out_specs=[pl.BlockSpec(memory_space=pltpu.VMEM)] * (half - 1),
-        scratch_shapes=[pltpu.SemaphoreType.DMA((half - 1,))],
+        out_specs=[pl.BlockSpec(memory_space=pltpu.VMEM)] * half,
+        scratch_shapes=[pltpu.SemaphoreType.DMA((half,))],
         compiler_params=pltpu.CompilerParams(vmem_limit_bytes=8 * 2**20),
-        cost_estimate=pl.CostEstimate(flops=0, bytes_accessed=4 * 2**20, transcendentals=0),
+        cost_estimate=pl.CostEstimate(flops=0, bytes_accessed=0, transcendentals=0),
         name="pick",
     )(place, rows, source)
 
@@ -149,10 +149,29 @@
     return jnp.asarray(take, jnp.bfloat16)
 
 
+def stage_kernel(source, out, sem):
+    copy = pltpu.make_async_copy(source, out, sem)
+    copy.start()
+    copy.wait()
+
+
+def stage(weights):
+    return pl.pallas_call(
+        stage_kernel,
+        out_shape=jax.ShapeDtypeStruct(weights.shape, weights.dtype),
+        in_specs=[pl.BlockSpec(memory_space=pl.ANY)],
+        out_specs=pl.BlockSpec(memory_space=pltpu.VMEM),
+        scratch_shapes=[pltpu.SemaphoreType.DMA],
+        compiler_params=pltpu.CompilerParams(vmem_limit_bytes=12 * 2**20),
+        cost_estimate=pl.CostEstimate(flops=0, bytes_accessed=0, transcendentals=0),
+        name="stage",
+    )(weights)
+
+
 def conv_kernel(plan, first, width, is_first, is_last, *refs):
     half, capacity, paired, counts = plan
-    live_ref, place, asked, fills, weights = refs[:5]
-    refs = refs[5:]
+    live_ref, place, fills, weights = refs[:4]
+    refs = refs[4:]
     groups = []
     for count in counts:
         groups.append(refs[:count])
@@ -195,11 +214,10 @@
                 spot = fills[at]
                 if not paired:
                     source = groups[side][0].at[r * capacity + k]
-                elif r == 0:
-                    begin = first if side == 0 else 0
-                    source = groups[side][0].at[asked[at], :, :, pl.ds(begin, width)]
                 else:
                     source = groups[side][r].at[k]
+                if side == 0:
+                    source = source.at[:, :, pl.ds(first, width)]
 
                 @pl.when(spot >= 0)
                 def _():
@@ -223,8 +241,7 @@
         lax.fori_loop(live, result.shape[0], erase, 0)
 
     def arrive(tile):
-        for _ in range(slot_count):
-            bring(window.at[tile, 0, pl.ds(0, PH), pl.ds(0, PW), :], tile, 0).wait()
+        pltpu.make_async_copy(window.at[tile], window.at[tile], sem.at[tile]).wait()
         if not is_first:
             fetch(tile).wait()
 
@@ -237,30 +254,31 @@
         else:
             result[tile] = conv
 
-    def finish(tile):
-        if not is_last:
-            return []
-
+    def finish(tile, slot):
         def put(values):
             result[tile] = values
 
-        return finish_steps(
-            lambda: sums[tile % 2], take[...], bias[...], gain[...], shift[...], put
-        )
-
-    arrive(0)
-    convolve(0)
+        return finish_steps(lambda: sums[slot], take[...], bias[...], gain[...], shift[...], put)
 
     def decode(tile, carry):
         arrive(tile)
-        convolve(tile, finish(tile - 1))
-        store(tile - 1).start()
+        if is_last:
+            convolve(tile, finish(jnp.maximum(tile - 1, 0), (tile + 1) % 2))
+
+            @pl.when(tile > 0)
+            def _():
+                store(tile - 1).start()
+
+        else:
+            convolve(tile)
+            store(tile).start()
         return carry
 
-    lax.fori_loop(1, live, decode, 0)
-    for step in finish(live - 1):
-        step()
-    store(live - 1).start()
+    lax.fori_loop(0, live, decode, 0)
+    if is_last:
+        for step in finish(live - 1, (live - 1) % 2):
+            step()
+        store(live - 1).start()
 
     def drain(tile, carry):
         store(tile).wait()
@@ -314,7 +332,7 @@
         out_specs=hbm,
         scratch_shapes=scratch,
         compiler_params=pltpu.CompilerParams(vmem_limit_bytes=24 * 2**20),
-        cost_estimate=pl.CostEstimate(flops=flops, bytes_accessed=8 * 2**20, transcendentals=0),
+        cost_estimate=pl.CostEstimate(flops=flops, bytes_accessed=0, transcendentals=0),
         name="conv_last" if is_last else "conv_part",
     )(*args)
 
@@ -322,7 +340,7 @@
 def decode_tiles(panels, tile_panels, tile_count, conv_weight, conv_bias, norm_gain, norm_shift):
     devices = lax.axis_size("dec")
     tile_rows, slot_count = tile_panels.shape
-    per_device, cells, _ = panels.shape
+    per_device, cells, channels = panels.shape
     capacity = max(1, tile_rows * slot_count // devices)
     half = devices // 2
     paired = half <= 8 and half & (half - 1) == 0
@@ -356,24 +374,23 @@
             landed = lax.all_to_all(picked, "dec", 0, 0, tiled=True, axis_index_groups=halves)
             return [landed.reshape(-1, PH, PW, width)]
         picked = pick(place, rows, source, half, capacity, which, first, width)
-        landed = [source.reshape(-1, PH, PW, source.shape[2])]
+        landed = [picked[0].reshape(capacity, PH, PW, width)]
         for r in range(1, half):
             pairs = [(d, d // half * half + (d % half ^ r)) for d in range(devices)]
-            moved = lax.ppermute(picked[r - 1], "dec", pairs)
+            moved = lax.ppermute(picked[r], "dec", pairs)
             landed.append(moved.reshape(capacity, PH, PW, width))
         return landed
 
     tail = [taken_cells(), *(v.reshape(1, C_OUT) for v in (conv_bias, norm_gain, norm_shift))]
-    scalars = (tile_count, place, asked, fills)
-    own = []
-    for first, width in zip(firsts, SPLIT):
-        own.append(exchange(panels, 0, first, width))
+    scalars = (tile_count, place, fills)
+    own = exchange(panels, 0, 0, channels)
+    weights = stage(conv_weight)
     partial = None
     for n, (first, width) in enumerate(zip(firsts, SPLIT)):
         brought = exchange(far[n], 1, 0, width)
-        plan = (half, capacity, paired, (len(own[n]), len(brought)))
+        plan = (half, capacity, paired, (len(own), len(brought)))
         partial = conv_step(
-            plan, first, width, scalars, conv_weight, [*own[n], *brought], partial,
+            plan, first, width, scalars, weights, [*own, *brought], partial,
             tail if n == len(SPLIT) - 1 else None, tile_rows,
         )
     return partial

time: 120 us -> 109 us (0.908)
  starting transfers between devices: 42.4 us -> 32.4 us
  Pallas kernels: 29.9 us -> 32.4 us
  local copies, waits for them, and re-layouts: 10.6 us -> 8.19 us
    ppermute x28 -> x21, starting transfers between devices: 34.4 us -> 24.4 us  [exchange(): moved = lax.ppermute(picked[r], 'dec', pairs)]
    ppermute x2, waiting for transfers between devices: 4.36 us -> 0.45 us  [decode_tiles(): far.append(lax.ppermute(source[:, :, first:first + width], 'dec', swap))]
    ppermute x28 -> x21, waiting for transfers between devices: 23 us -> 26.8 us  [exchange(): moved = lax.ppermute(picked[r], 'dec', pairs)]
    unnamed x16 -> x12, local copies, waits for them, and re-layouts: 6.69 us -> 4.24 us
    pallas_call x4 -> x3, Pallas kernels: 5.69 us -> 7.76 us  [pick(): pl.pallas_call(functools.partial(pick_kernel, half, capacity, which, firs...]
  transfers between devices with their start and end apart: 31 -> 24, of which waited for: 12 -> 9; matrix products, arithmetic and copies ran while one was open for 3% -> 3% of each run, Pallas kernels for 14% -> 18%
where the time goes in v2:
time: 109 us
  waiting for transfers between devices  34.6 us (32%)
  starting transfers between devices  32.4 us (30%)
  Pallas kernels  32.4 us (30%)
  local copies, waits for them, and re-layouts  8.19 us (8%)
    ppermute x21, waiting for transfers between devices, exchange(): moved = lax.ppermute(picked[r], 'dec', pairs)  26.8 us
    ppermute x21, starting transfers between devices, exchange(): moved = lax.ppermute(picked[r], 'dec', pairs)  24.4 us
    pallas_call x2, Pallas kernels, conv_step(): pl.pallas_call(functools.partial(conv_kernel, plan, first, width, is_firs...  24.1 us
    pallas_call x3, Pallas kernels, pick(): pl.pallas_call(functools.partial(pick_kernel, half, capacity, which, firs...  7.76 us
    all_to_all x1, waiting for transfers between devices, decode_tiles(): lax.all_to_all(sent, 'dec', 0, 0, tiled=True, axis_index_groups=halves)  7.27 us
    all_to_all x1, starting transfers between devices, decode_tiles(): lax.all_to_all(sent, 'dec', 0, 0, tiled=True, axis_index_groups=halves)  4.73 us
    unnamed x12, local copies, waits for them, and re-layouts  4.24 us
    ppermute x2, starting transfers between devices, decode_tiles(): far.append(lax.ppermute(source[:, :, first:first + width], 'dec', swap))  3.29 us
  transfers between devices with their start and end apart: 24, of which 9 were waited for; matrix products, arithmetic and copies ran while one was open for 3% of the time, Pallas kernels for 18%

profile of v2, /device:TPU:21, one launch (start us, length us, event | category | flops | bytes accessed | tf_op | source)
XLA Modules:
  0.0 108.8 jit_solution(15401294144216188264)
XLA Ops:
  3.9 4.7 %all-to-all-start = ((s32[8,2,4]{2,1,0:T(2,128)}), s32[8,2,4]{2,1,0:T(2,128)S(1)}, u32[]{:S(2)}, u32[]{:S(2)}) async-start(s32[8,2,4]{2,1,0:T(2,128)} %copy.20), calls=%async_computation | async-start | bytes 16384 | tf_op jit(solution)/shard_map/all_to_all | solution.py:357
  8.7 7.3 %all-to-all-done = s32[8,2,4]{2,1,0:T(2,128)S(1)} async-done(((s32[8,2,4]{2,1,0:T(2,128)}), s32[8,2,4]{2,1,0:T(2,128)S(1)}, u32[]{:S(2)}, u32[]{:S(2)}) %all-to-all-start) | async-done | bytes 288 | tf_op jit(solution)/shard_map/all_to_all | solution.py:357
  17.3 3.5 %pick.3 = (bf16[4,64,512]{2,1,0:T(8,128)(2,1)S(1)}, bf16[4,64,512]{2,1,0:T(8,128)(2,1)S(1)}, bf16[4,64,512]{2,1,0:T(8,128)(2,1)S(1)}, bf16[4,64,512]{2,1,0:T(8,1...) custom-call(s32[2]{0:T(128)S(1)} %pad_add_fusion.1.place.refs_1_, ...), custom_call_target="tpu_custom_call" | custom-call | tf_op jit(solution)/shard_map/pick/pallas_call | solution.py:67
  20.9 1.8 %collective-permute-start.5 = (bf16[4,64,512]{2,1,0:T(8,128)(2,1)S(1)}, bf16[4,64,512]{2,1,0:T(8,128)(2,1)S(1)}, u32[]{:S(2)}, u32[]{:S(2)}) collective-permute-start(bf16[4,64,512]{2,1,0:T(8,128)(2,1)S(1)} %get-tuple-element.37), channel_id=1, source_target_pairs={{0,6},{1,7},{2,4},{3,5},{4,2},{5,3},{6,0},{7,1},{8,14},{9,15},{10,... | collective-permute-start | bytes 786440 | tf_op jit(solution)/shard_map/ppermute | solution.py:380
  24.2 3.2 %collective-permute-start.8 = (bf16[16,64,256]{2,1,0:T(8,128)(2,1)S(1)}, bf16[16,64,256]{2,1,0:T(8,128)(2,1)S(1)}, u32[]{:S(2)}, u32[]{:S(2)}) collective-permute-start(bf16[16,64,256]{2,1,0:T(8,128)(2,1)S(1)} %slice.7), channel_id=1, source_target_pairs={{0,8},{1,9},{2,10},{3,11},{4,12},{5,13},{6,14},{7,15},{8,0},{9,1},... | collective-permute-start | bytes 1572872 | tf_op jit(solution)/shard_map/ppermute | solution.py:365
  27.4 3.6 %collective-permute-start.6 = (bf16[4,64,512]{2,1,0:T(8,128)(2,1)S(1)}, bf16[4,64,512]{2,1,0:T(8,128)(2,1)S(1)}, u32[]{:S(2)}, u32[]{:S(2)}) collective-permute-start(bf16[4,64,512]{2,1,0:T(8,128)(2,1)S(1)} %get-tuple-element.38), channel_id=1, source_target_pairs={{0,7},{1,6},{2,5},{3,4},{4,3},{5,2},{6,1},{7,0},{8,15},{9,14},{10,... | collective-permute-start | bytes 786440 | tf_op jit(solution)/shard_map/ppermute | solution.py:380
  30.9 4.9 %collective-permute-done.4 = bf16[4,64,512]{2,1,0:T(8,128)(2,1)S(1)} collective-permute-done((bf16[4,64,512]{2,1,0:T(8,128)(2,1)S(1)}, bf16[4,64,512]{2,1,0:T(8,128)(2,1)S(1)}, u32[]{:S(2)}, u32[]{:S(2)}) %collective-permute-start.4) | collective-permute-done | bytes 262176 | tf_op jit(solution)/shard_map/ppermute | solution.py:380
  36.2 5.5 %collective-permute-done.5 = bf16[4,64,512]{2,1,0:T(8,128)(2,1)S(1)} collective-permute-done((bf16[4,64,512]{2,1,0:T(8,128)(2,1)S(1)}, bf16[4,64,512]{2,1,0:T(8,128)(2,1)S(1)}, u32[]{:S(2)}, u32[]{:S(2)}) %collective-permute-start.5) | collective-permute-done | bytes 262176 | tf_op jit(solution)/shard_map/ppermute | solution.py:380
  42.4 11.8 %collective-permute-done.6 = bf16[4,64,512]{2,1,0:T(8,128)(2,1)S(1)} collective-permute-done((bf16[4,64,512]{2,1,0:T(8,128)(2,1)S(1)}, bf16[4,64,512]{2,1,0:T(8,128)(2,1)S(1)}, u32[]{:S(2)}, u32[]{:S(2)}) %collective-permute-start.6) | collective-permute-done | bytes 262176 | tf_op jit(solution)/shard_map/ppermute | solution.py:380
  54.1 3.3 %collective-permute-start.3 = (bf16[4,64,512]{2,1,0:T(8,128)(2,1)S(1)}, bf16[4,64,512]{2,1,0:T(8,128)(2,1)S(1)}, u32[]{:S(2)}, u32[]{:S(2)}) collective-permute-start(bf16[4,64,512]{2,1,0:T(8,128)(2,1)S(1)} %get-tuple-element.35), channel_id=1, source_target_pairs={{0,4},{1,5},{2,6},{3,7},{4,0},{5,1},{6,2},{7,3},{8,12},{9,13},{10,... | collective-permute-start | bytes 786440 | tf_op jit(solution)/shard_map/ppermute | solution.py:380
  57.4 2.1 %pick.5 = (bf16[4,64,256]{2,1,0:T(8,128)(2,1)S(1)}, bf16[4,64,256]{2,1,0:T(8,128)(2,1)S(1)}, bf16[4,64,256]{2,1,0:T(8,128)(2,1)S(1)}, bf16[4,64,256]{2,1,0:T(8,1...) custom-call(s32[2]{0:T(128)S(1)} %pad_add_fusion.1.place.refs_1_, ...), custom_call_target="tpu_custom_call" | custom-call | tf_op jit(solution)/shard_map/pick/pallas_call | solution.py:67
  60.7 1.5 %collective-permute-start.18 = (bf16[4,64,256]{2,1,0:T(8,128)(2,1)S(1)}, bf16[4,64,256]{2,1,0:T(8,128)(2,1)S(1)}, u32[]{:S(2)}, u32[]{:S(2)}) collective-permute-start(bf16[4,64,256]{2,1,0:T(8,128)(2,1)S(1)} %get-tuple-element.52), channel_id=1, source_target_pairs={{0,3},{1,2},{2,1},{3,0},{4,7},{5,6},{6,5},{7,4},{8,11},{9,10},{10,... | collective-permute-start | bytes 393224 | tf_op jit(solution)/shard_map/ppermute | solution.py:380
  62.1 3.0 %copy-done = bf16[3,3,3,512,256]{4,3,2,1,0:T(8,128)(2,1)S(1)} copy-done((bf16[3,3,3,512,256]{4,3,2,1,0:T(8,128)(2,1)S(1)}, bf16[3,3,3,512,256]{4,3,2,1,0:T(8,128)(2,1)}, u32[]{:S(2)}) %copy-start) | copy-done | bytes 7077912
  65.6 2.1 %pick.4 = (bf16[4,64,256]{2,1,0:T(8,128)(2,1)S(1)}, bf16[4,64,256]{2,1,0:T(8,128)(2,1)S(1)}, bf16[4,64,256]{2,1,0:T(8,128)(2,1)S(1)}, bf16[4,64,256]{2,1,0:T(8,1...) custom-call(s32[2]{0:T(128)S(1)} %pad_add_fusion.1.place.refs_1_, ...), custom_call_target="tpu_custom_call" | custom-call | tf_op jit(solution)/shard_map/pick/pallas_call | solution.py:67
  67.8 1.8 %collective-permute-start.20 = (bf16[4,64,256]{2,1,0:T(8,128)(2,1)S(1)}, bf16[4,64,256]{2,1,0:T(8,128)(2,1)S(1)}, u32[]{:S(2)}, u32[]{:S(2)}) collective-permute-start(bf16[4,64,256]{2,1,0:T(8,128)(2,1)S(1)} %get-tuple-element.54), channel_id=1, source_target_pairs={{0,5},{1,4},{2,7},{3,6},{4,1},{5,0},{6,3},{7,2},{8,13},{9,12},{10,... | collective-permute-start | bytes 393224 | tf_op jit(solution)/shard_map/ppermute | solution.py:380
  69.6 2.6 %collective-permute-start.22 = (bf16[4,64,256]{2,1,0:T(8,128)(2,1)S(1)}, bf16[4,64,256]{2,1,0:T(8,128)(2,1)S(1)}, u32[]{:S(2)}, u32[]{:S(2)}) collective-permute-start(bf16[4,64,256]{2,1,0:T(8,128)(2,1)S(1)} %get-tuple-element.56), channel_id=1, source_target_pairs={{0,7},{1,6},{2,5},{3,4},{4,3},{5,2},{6,1},{7,0},{8,15},{9,14},{10,... | collective-permute-start | bytes 393224 | tf_op jit(solution)/shard_map/ppermute | solution.py:380
  72.7 1.3 %collective-permute-done.20 = bf16[4,64,256]{2,1,0:T(8,128)(2,1)S(1)} collective-permute-done((bf16[4,64,256]{2,1,0:T(8,128)(2,1)S(1)}, bf16[4,64,256]{2,1,0:T(8,128)(2,1)S(1)}, u32[]{:S(2)}, u32[]{:S(2)}) %collective-permute-start.20) | collective-permute-done | bytes 131104 | tf_op jit(solution)/shard_map/ppermute | solution.py:380
  74.5 1.7 %collective-permute-done.21 = bf16[4,64,256]{2,1,0:T(8,128)(2,1)S(1)} collective-permute-done((bf16[4,64,256]{2,1,0:T(8,128)(2,1)S(1)}, bf16[4,64,256]{2,1,0:T(8,128)(2,1)S(1)}, u32[]{:S(2)}, u32[]{:S(2)}) %collective-permute-start.21) | collective-permute-done | bytes 131104 | tf_op jit(solution)/shard_map/ppermute | solution.py:380
  76.2 1.5 %collective-permute-start.12 = (bf16[4,64,256]{2,1,0:T(8,128)(2,1)S(1)}, bf16[4,64,256]{2,1,0:T(8,128)(2,1)S(1)}, u32[]{:S(2)}, u32[]{:S(2)}) collective-permute-start(bf16[4,64,256]{2,1,0:T(8,128)(2,1)S(1)} %get-tuple-element.44), channel_id=1, source_target_pairs={{0,4},{1,5},{2,6},{3,7},{4,0},{5,1},{6,2},{7,3},{8,12},{9,13},{10,... | collective-permute-start | bytes 393224 | tf_op jit(solution)/shard_map/ppermute | solution.py:380
  77.7 1.4 %collective-permute-done.22 = bf16[4,64,256]{2,1,0:T(8,128)(2,1)S(1)} collective-permute-done((bf16[4,64,256]{2,1,0:T(8,128)(2,1)S(1)}, bf16[4,64,256]{2,1,0:T(8,128)(2,1)S(1)}, u32[]{:S(2)}, u32[]{:S(2)}) %collective-permute-start.22) | collective-permute-done | bytes 131104 | tf_op jit(solution)/shard_map/ppermute | solution.py:380
  79.1 1.7 %collective-permute-start.13 = (bf16[4,64,256]{2,1,0:T(8,128)(2,1)S(1)}, bf16[4,64,256]{2,1,0:T(8,128)(2,1)S(1)}, u32[]{:S(2)}, u32[]{:S(2)}) collective-permute-start(bf16[4,64,256]{2,1,0:T(8,128)(2,1)S(1)} %get-tuple-element.45), channel_id=1, source_target_pairs={{0,5},{1,4},{2,7},{3,6},{4,1},{5,0},{6,3},{7,2},{8,13},{9,12},{10,... | collective-permute-start | bytes 393224 | tf_op jit(solution)/shard_map/ppermute | solution.py:380
  82.0 2.6 %collective-permute-start.15 = (bf16[4,64,256]{2,1,0:T(8,128)(2,1)S(1)}, bf16[4,64,256]{2,1,0:T(8,128)(2,1)S(1)}, u32[]{:S(2)}, u32[]{:S(2)}) collective-permute-start(bf16[4,64,256]{2,1,0:T(8,128)(2,1)S(1)} %get-tuple-element.47), channel_id=1, source_target_pairs={{0,7},{1,6},{2,5},{3,4},{4,3},{5,2},{6,1},{7,0},{8,15},{9,14},{10,... | collective-permute-start | bytes 393224 | tf_op jit(solution)/shard_map/ppermute | solution.py:380
  84.6 11.0 %conv_part.1.refs_20_ = f32[4,448,256]{2,1,0:T(8,128)S(1)} custom-call(s32[1]{0:T(128)} %copy.21.refs_0_, s32[2]{0:T(128)S(1)} %pad_add_fusion.1.place.refs_1_, s32[64]{0:T(128)S(1)} %fusion.3.refs_2_, bf16[3,3,3,512,256]{4,3,2,1,0:T(8,128)(2,1)S(1)} %stage.1.refs_3_, bf16[4,8,8,512]{3,2,1,0:T(8,128)(2,1)S(1)} %bitcast.33, ...), custom_call_target="tpu_custom_call" | custom-call | flops 6341787648 | tf_op jit(solution)/shard_map/conv_part/pallas_call | solution.py:328
  95.7 13.1 %conv_last.1 = bf16[4,392,256]{2,1,0:T(8,128)(2,1)} custom-call(s32[1]{0:T(128)} %copy.21.refs_0_, s32[2]{0:T(128)S(1)} %pad_add_fusion.1.place.refs_1_, s32[64]{0:T(128)S(1)} %fusion.3.refs_2_, bf16[3,3,3,512,256]{4,3,2,1,0:T(8,128)(2,1)S(1)} %stage.1.refs_3_, bf16[4,8,8,512]{3,2,1,0:T(8,128)(2,1)S(1)} %bitcast.34, bf16[4,8,8,512]{3,2,1,0:T(8,128)(2,1)S(1)} %bitcast.42, ...), custom_call_target="tpu_custom_call" | custom-call | flops 6341787648 | tf_op jit(solution)/shard_map/conv_last/pallas_call | solution.py:328
  (59 shorter events, 11.0 us)
Async XLA Ops:
  1.1 22.0 %collective-permute-start.7 = (bf16[16,64,256]{2,1,0:T(8,128)(2,1)S(1)}, bf16[16,64,256]{2,1,0:T(8,128)(2,1)S(1)}, u32[]{:S(2)}, u32[]{:S(2)}) collective-permute-start(bf16[16,64,256]{2,1,0:T(8,128)(2,1)S(1)} %slice.6), channel_id=1, source_target_pairs={{0,8},{1,9},{2,10},{3,11},{4,12},{5,13},{6,14},{7,15},{8,0},{9,1},... | collective-permute-start | bytes 1572872 | tf_op jit(solution)/shard_map/ppermute | solution.py:365
  3.9 12.1 %all-to-all-start = ((s32[8,2,4]{2,1,0:T(2,128)}), s32[8,2,4]{2,1,0:T(2,128)S(1)}, u32[]{:S(2)}, u32[]{:S(2)}) async-start(s32[8,2,4]{2,1,0:T(2,128)} %copy.20), calls=%async_computation | async-start | bytes 16384 | tf_op jit(solution)/shard_map/all_to_all | solution.py:357
  20.8 15.1 %collective-permute-start.4 = (bf16[4,64,512]{2,1,0:T(8,128)(2,1)S(1)}, bf16[4,64,512]{2,1,0:T(8,128)(2,1)S(1)}, u32[]{:S(2)}, u32[]{:S(2)}) collective-permute-start(bf16[4,64,512]{2,1,0:T(8,128)(2,1)S(1)} %get-tuple-element.36), channel_id=1, source_target_pairs={{0,5},{1,4},{2,7},{3,6},{4,1},{5,0},{6,3},{7,2},{8,13},{9,12},{10,... | collective-permute-start | bytes 786440 | tf_op jit(solution)/shard_map/ppermute | solution.py:380
  20.9 20.8 %collective-permute-start.5 = (bf16[4,64,512]{2,1,0:T(8,128)(2,1)S(1)}, bf16[4,64,512]{2,1,0:T(8,128)(2,1)S(1)}, u32[]{:S(2)}, u32[]{:S(2)}) collective-permute-start(bf16[4,64,512]{2,1,0:T(8,128)(2,1)S(1)} %get-tuple-element.37), channel_id=1, source_target_pairs={{0,6},{1,7},{2,4},{3,5},{4,2},{5,3},{6,0},{7,1},{8,14},{9,15},{10,... | collective-permute-start | bytes 786440 | tf_op jit(solution)/shard_map/ppermute | solution.py:380
  24.2 37.9 %collective-permute-start.8 = (bf16[16,64,256]{2,1,0:T(8,128)(2,1)S(1)}, bf16[16,64,256]{2,1,0:T(8,128)(2,1)S(1)}, u32[]{:S(2)}, u32[]{:S(2)}) collective-permute-start(bf16[16,64,256]{2,1,0:T(8,128)(2,1)S(1)} %slice.7), channel_id=1, source_target_pairs={{0,8},{1,9},{2,10},{3,11},{4,12},{5,13},{6,14},{7,15},{8,0},{9,1},... | collective-permute-start | bytes 1572872 | tf_op jit(solution)/shard_map/ppermute | solution.py:365
  27.4 26.8 %collective-permute-start.6 = (bf16[4,64,512]{2,1,0:T(8,128)(2,1)S(1)}, bf16[4,64,512]{2,1,0:T(8,128)(2,1)S(1)}, u32[]{:S(2)}, u32[]{:S(2)}) collective-permute-start(bf16[4,64,512]{2,1,0:T(8,128)(2,1)S(1)} %get-tuple-element.38), channel_id=1, source_target_pairs={{0,7},{1,6},{2,5},{3,4},{4,3},{5,2},{6,1},{7,0},{8,15},{9,14},{10,... | collective-permute-start | bytes 786440 | tf_op jit(solution)/shard_map/ppermute | solution.py:380
  30.9 28.6 %collective-permute-start = (bf16[4,64,512]{2,1,0:T(8,128)(2,1)S(1)}, bf16[4,64,512]{2,1,0:T(8,128)(2,1)S(1)}, u32[]{:S(2)}, u32[]{:S(2)}) collective-permute-start(bf16[4,64,512]{2,1,0:T(8,128)(2,1)S(1)} %get-tuple-element.32), channel_id=1, source_target_pairs={{0,1},{1,0},{2,3},{3,2},{4,5},{5,4},{6,7},{7,6},{8,9},{9,8},{10,11... | collective-permute-start | bytes 786440 | tf_op jit(solution)/shard_map/ppermute | solution.py:380
  35.9 24.5 %collective-permute-start.1 = (bf16[4,64,512]{2,1,0:T(8,128)(2,1)S(1)}, bf16[4,64,512]{2,1,0:T(8,128)(2,1)S(1)}, u32[]{:S(2)}, u32[]{:S(2)}) collective-permute-start(bf16[4,64,512]{2,1,0:T(8,128)(2,1)S(1)} %get-tuple-element.33), channel_id=1, source_target_pairs={{0,2},{1,3},{2,0},{3,1},{4,6},{5,7},{6,4},{7,5},{8,10},{9,11},{10,... | collective-permute-start | bytes 786440 | tf_op jit(solution)/shard_map/ppermute | solution.py:380
  41.7 19.0 %collective-permute-start.2 = (bf16[4,64,512]{2,1,0:T(8,128)(2,1)S(1)}, bf16[4,64,512]{2,1,0:T(8,128)(2,1)S(1)}, u32[]{:S(2)}, u32[]{:S(2)}) collective-permute-start(bf16[4,64,512]{2,1,0:T(8,128)(2,1)S(1)} %get-tuple-element.34), channel_id=1, source_target_pairs={{0,3},{1,2},{2,1},{3,0},{4,7},{5,6},{6,5},{7,4},{8,11},{9,10},{10,... | collective-permute-start | bytes 786440 | tf_op jit(solution)/shard_map/ppermute | solution.py:380
  54.1 13.6 %collective-permute-start.3 = (bf16[4,64,512]{2,1,0:T(8,128)(2,1)S(1)}, bf16[4,64,512]{2,1,0:T(8,128)(2,1)S(1)}, u32[]{:S(2)}, u32[]{:S(2)}) collective-permute-start(bf16[4,64,512]{2,1,0:T(8,128)(2,1)S(1)} %get-tuple-element.35), channel_id=1, source_target_pairs={{0,4},{1,5},{2,6},{3,7},{4,0},{5,1},{6,2},{7,3},{8,12},{9,13},{10,... | collective-permute-start | bytes 786440 | tf_op jit(solution)/shard_map/ppermute | solution.py:380
  59.6 10.1 %collective-permute-start.16 = (bf16[4,64,256]{2,1,0:T(8,128)(2,1)S(1)}, bf16[4,64,256]{2,1,0:T(8,128)(2,1)S(1)}, u32[]{:S(2)}, u32[]{:S(2)}) collective-permute-start(bf16[4,64,256]{2,1,0:T(8,128)(2,1)S(1)} %get-tuple-element.50), channel_id=1, source_target_pairs={{0,1},{1,0},{2,3},{3,2},{4,5},{5,4},{6,7},{7,6},{8,9},{9,8},{10,11... | collective-permute-start | bytes 393224 | tf_op jit(solution)/shard_map/ppermute | solution.py:380
  60.4 9.2 %collective-permute-start.17 = (bf16[4,64,256]{2,1,0:T(8,128)(2,1)S(1)}, bf16[4,64,256]{2,1,0:T(8,128)(2,1)S(1)}, u32[]{:S(2)}, u32[]{:S(2)}) collective-permute-start(bf16[4,64,256]{2,1,0:T(8,128)(2,1)S(1)} %get-tuple-element.51), channel_id=1, source_target_pairs={{0,2},{1,3},{2,0},{3,1},{4,6},{5,7},{6,4},{7,5},{8,10},{9,11},{10,... | collective-permute-start | bytes 393224 | tf_op jit(solution)/shard_map/ppermute | solution.py:380
  60.7 11.6 %collective-permute-start.18 = (bf16[4,64,256]{2,1,0:T(8,128)(2,1)S(1)}, bf16[4,64,256]{2,1,0:T(8,128)(2,1)S(1)}, u32[]{:S(2)}, u32[]{:S(2)}) collective-permute-start(bf16[4,64,256]{2,1,0:T(8,128)(2,1)S(1)} %get-tuple-element.52), channel_id=1, source_target_pairs={{0,3},{1,2},{2,1},{3,0},{4,7},{5,6},{6,5},{7,4},{8,11},{9,10},{10,... | collective-permute-start | bytes 393224 | tf_op jit(solution)/shard_map/ppermute | solution.py:380
  62.1 10.3 %collective-permute-start.19 = (bf16[4,64,256]{2,1,0:T(8,128)(2,1)S(1)}, bf16[4,64,256]{2,1,0:T(8,128)(2,1)S(1)}, u32[]{:S(2)}, u32[]{:S(2)}) collective-permute-start(bf16[4,64,256]{2,1,0:T(8,128)(2,1)S(1)} %get-tuple-element.53), channel_id=1, source_target_pairs={{0,4},{1,5},{2,6},{3,7},{4,0},{5,1},{6,2},{7,3},{8,12},{9,13},{10,... | collective-permute-start | bytes 393224 | tf_op jit(solution)/shard_map/ppermute | solution.py:380
  67.8 6.2 %collective-permute-start.20 = (bf16[4,64,256]{2,1,0:T(8,128)(2,1)S(1)}, bf16[4,64,256]{2,1,0:T(8,128)(2,1)S(1)}, u32[]{:S(2)}, u32[]{:S(2)}) collective-permute-start(bf16[4,64,256]{2,1,0:T(8,128)(2,1)S(1)} %get-tuple-element.54), channel_id=1, source_target_pairs={{0,5},{1,4},{2,7},{3,6},{4,1},{5,0},{6,3},{7,2},{8,13},{9,12},{10,... | collective-permute-start | bytes 393224 | tf_op jit(solution)/shard_map/ppermute | solution.py:380
  69.6 6.6 %collective-permute-start.21 = (bf16[4,64,256]{2,1,0:T(8,128)(2,1)S(1)}, bf16[4,64,256]{2,1,0:T(8,128)(2,1)S(1)}, u32[]{:S(2)}, u32[]{:S(2)}) collective-permute-start(bf16[4,64,256]{2,1,0:T(8,128)(2,1)S(1)} %get-tuple-element.55), channel_id=1, source_target_pairs={{0,6},{1,7},{2,4},{3,5},{4,2},{5,3},{6,0},{7,1},{8,14},{9,15},{10,... | collective-permute-start | bytes 393224 | tf_op jit(solution)/shard_map/ppermute | solution.py:380
  69.6 9.5 %collective-permute-start.22 = (bf16[4,64,256]{2,1,0:T(8,128)(2,1)S(1)}, bf16[4,64,256]{2,1,0:T(8,128)(2,1)S(1)}, u32[]{:S(2)}, u32[]{:S(2)}) collective-permute-start(bf16[4,64,256]{2,1,0:T(8,128)(2,1)S(1)} %get-tuple-element.56), channel_id=1, source_target_pairs={{0,7},{1,6},{2,5},{3,4},{4,3},{5,2},{6,1},{7,0},{8,15},{9,14},{10,... | collective-permute-start | bytes 393224 | tf_op jit(solution)/shard_map/ppermute | solution.py:380
  72.3 8.6 %collective-permute-start.9 = (bf16[4,64,256]{2,1,0:T(8,128)(2,1)S(1)}, bf16[4,64,256]{2,1,0:T(8,128)(2,1)S(1)}, u32[]{:S(2)}, u32[]{:S(2)}) collective-permute-start(bf16[4,64,256]{2,1,0:T(8,128)(2,1)S(1)} %get-tuple-element.41), channel_id=1, source_target_pairs={{0,1},{1,0},{2,3},{3,2},{4,5},{5,4},{6,7},{7,6},{8,9},{9,8},{10,11... | collective-permute-start | bytes 393224 | tf_op jit(solution)/shard_map/ppermute | solution.py:380
  72.4 9.6 %collective-permute-start.10 = (bf16[4,64,256]{2,1,0:T(8,128)(2,1)S(1)}, bf16[4,64,256]{2,1,0:T(8,128)(2,1)S(1)}, u32[]{:S(2)}, u32[]{:S(2)}) collective-permute-start(bf16[4,64,256]{2,1,0:T(8,128)(2,1)S(1)} %get-tuple-element.42), channel_id=1, source_target_pairs={{0,2},{1,3},{2,0},{3,1},{4,6},{5,7},{6,4},{7,5},{8,10},{9,11},{10,... | collective-permute-start | bytes 393224 | tf_op jit(solution)/shard_map/ppermute | solution.py:380
  74.0 21.6 %collective-permute-start.11 = (bf16[4,64,256]{2,1,0:T(8,128)(2,1)S(1)}, bf16[4,64,256]{2,1,0:T(8,128)(2,1)S(1)}, u32[]{:S(2)}, u32[]{:S(2)}) collective-permute-start(bf16[4,64,256]{2,1,0:T(8,128)(2,1)S(1)} %get-tuple-element.43), channel_id=1, source_target_pairs={{0,3},{1,2},{2,1},{3,0},{4,7},{5,6},{6,5},{7,4},{8,11},{9,10},{10,... | collective-permute-start | bytes 393224 | tf_op jit(solution)/shard_map/ppermute | solution.py:380
  76.2 19.4 %collective-permute-start.12 = (bf16[4,64,256]{2,1,0:T(8,128)(2,1)S(1)}, bf16[4,64,256]{2,1,0:T(8,128)(2,1)S(1)}, u32[]{:S(2)}, u32[]{:S(2)}) collective-permute-start(bf16[4,64,256]{2,1,0:T(8,128)(2,1)S(1)} %get-tuple-element.44), channel_id=1, source_target_pairs={{0,4},{1,5},{2,6},{3,7},{4,0},{5,1},{6,2},{7,3},{8,12},{9,13},{10,... | collective-permute-start | bytes 393224 | tf_op jit(solution)/shard_map/ppermute | solution.py:380
  79.1 16.5 %collective-permute-start.13 = (bf16[4,64,256]{2,1,0:T(8,128)(2,1)S(1)}, bf16[4,64,256]{2,1,0:T(8,128)(2,1)S(1)}, u32[]{:S(2)}, u32[]{:S(2)}) collective-permute-start(bf16[4,64,256]{2,1,0:T(8,128)(2,1)S(1)} %get-tuple-element.45), channel_id=1, source_target_pairs={{0,5},{1,4},{2,7},{3,6},{4,1},{5,0},{6,3},{7,2},{8,13},{9,12},{10,... | collective-permute-start | bytes 393224 | tf_op jit(solution)/shard_map/ppermute | solution.py:380
  80.9 14.8 %collective-permute-start.14 = (bf16[4,64,256]{2,1,0:T(8,128)(2,1)S(1)}, bf16[4,64,256]{2,1,0:T(8,128)(2,1)S(1)}, u32[]{:S(2)}, u32[]{:S(2)}) collective-permute-start(bf16[4,64,256]{2,1,0:T(8,128)(2,1)S(1)} %get-tuple-element.46), channel_id=1, source_target_pairs={{0,6},{1,7},{2,4},{3,5},{4,2},{5,3},{6,0},{7,1},{8,14},{9,15},{10,... | collective-permute-start | bytes 393224 | tf_op jit(solution)/shard_map/ppermute | solution.py:380
  82.0 13.6 %collective-permute-start.15 = (bf16[4,64,256]{2,1,0:T(8,128)(2,1)S(1)}, bf16[4,64,256]{2,1,0:T(8,128)(2,1)S(1)}, u32[]{:S(2)}, u32[]{:S(2)}) collective-permute-start(bf16[4,64,256]{2,1,0:T(8,128)(2,1)S(1)} %get-tuple-element.47), channel_id=1, source_target_pairs={{0,7},{1,6},{2,5},{3,4},{4,3},{5,2},{6,1},{7,0},{8,15},{9,14},{10,... | collective-permute-start | bytes 393224 | tf_op jit(solution)/shard_map/ppermute | solution.py:380
  (6 other events, 48.5 us)

commit v3 on v2

--- a/solution.py
+++ b/solution.py
@@ -44,36 +44,40 @@
     return packed % per_device, packed // per_device - 1
 
 
-def pick_kernel(half, capacity, which, first, width, place, rows, source, *refs):
-    outs, sem = refs[:-1], refs[-1]
+def pick_kernel(capacity, which, partners, columns, place, rows, *refs):
+    count = len(columns)
+    sources, outs, sem = refs[:count], refs[count:-1], refs[-1]
     for begin in (True, False):
-        for r in range(half):
+        for n, r in enumerate(partners):
             q = place[1] ^ r
             for k in range(capacity):
                 row = rows[(q * 2 + which) * capacity + k]
-                copy = pltpu.make_async_copy(
-                    source.at[row, :, pl.ds(first, width)], outs[r].at[k], sem.at[r]
-                )
-                if begin:
-                    copy.start()
-                else:
-                    copy.wait()
-
-
-def pick(place, rows, source, half, capacity, which, first, width):
-    cells = source.shape[1]
+                for source, (first, width) in zip(sources, columns):
+                    copy = pltpu.make_async_copy(
+                        source.at[row], outs[n].at[k, :, pl.ds(first, width)], sem.at[n]
+                    )
+                    if begin:
+                        copy.start()
+                    else:
+                        copy.wait()
+
+
+def pick(place, rows, sources, capacity, which, partners):
+    cells = sources[0].shape[1]
+    widths = [source.shape[2] for source in sources]
+    columns = tuple((sum(widths[:n]), widths[n]) for n in range(len(widths)))
     smem = pl.BlockSpec(memory_space=pltpu.SMEM)
-    shape = jax.ShapeDtypeStruct((capacity, cells, width), jnp.bfloat16)
+    shape = jax.ShapeDtypeStruct((capacity, cells, sum(widths)), jnp.bfloat16)
     return pl.pallas_call(
-        functools.partial(pick_kernel, half, capacity, which, first, width),
-        out_shape=[shape] * half,
-        in_specs=[smem, smem, pl.BlockSpec(memory_space=pl.ANY)],
-        out_specs=[pl.BlockSpec(memory_space=pltpu.VMEM)] * half,
-        scratch_shapes=[pltpu.SemaphoreType.DMA((half,))],
+        functools.partial(pick_kernel, capacity, which, partners, columns),
+        out_shape=[shape] * len(partners),
+        in_specs=[smem, smem] + [pl.BlockSpec(memory_space=pl.ANY)] * len(sources),
+        out_specs=[pl.BlockSpec(memory_space=pltpu.VMEM)] * len(partners),
+        scratch_shapes=[pltpu.SemaphoreType.DMA((len(partners),))],
         compiler_params=pltpu.CompilerParams(vmem_limit_bytes=8 * 2**20),
         cost_estimate=pl.CostEstimate(flops=0, bytes_accessed=0, transcendentals=0),
         name="pick",
-    )(place, rows, source)
+    )(place, rows, *sources)
 
 
 def conv_tile(window, weights, tile, first, width, between=()):
@@ -337,10 +341,14 @@
     )(*args)
 
 
+def partner_sets(half):
+    return [tuple(range(half))]
+
+
 def decode_tiles(panels, tile_panels, tile_count, conv_weight, conv_bias, norm_gain, norm_shift):
     devices = lax.axis_size("dec")
     tile_rows, slot_count = tile_panels.shape
-    per_device, cells, channels = panels.shape
+    per_device, cells, _ = panels.shape
     capacity = max(1, tile_rows * slot_count // devices)
     half = devices // 2
     paired = half <= 8 and half & (half - 1) == 0
@@ -357,37 +365,41 @@
     got = lax.all_to_all(sent, "dec", 0, 0, tiled=True, axis_index_groups=halves)
 
     firsts = [sum(SPLIT[:n]) for n in range(len(SPLIT))]
+    parts = [panels[:, :, first : first + width] for first, width in zip(firsts, SPLIT)]
     far = []
-    source = panels
-    for first, width in zip(firsts, SPLIT):
+    for part in parts:
         if far:
-            source, far[-1] = lax.optimization_barrier((panels, far[-1]))
-        far.append(lax.ppermute(source[:, :, first : first + width], "dec", swap))
+            part, far[-1] = lax.optimization_barrier((part, far[-1]))
+        far.append(lax.ppermute(part, "dec", swap))
 
     rows = got.reshape(-1)
     place = jnp.stack([mine, seat])
 
-    def exchange(source, which, first, width):
+    def exchange(sources, which):
+        width = sum(source.shape[2] for source in sources)
         if not paired:
-            picked = source[got[:, which].reshape(-1), :, first : first + width]
+            source = sources[0] if len(sources) == 1 else panels
+            picked = source[got[:, which].reshape(-1)]
             picked = picked.reshape(half, capacity, cells, width)
             landed = lax.all_to_all(picked, "dec", 0, 0, tiled=True, axis_index_groups=halves)
             return [landed.reshape(-1, PH, PW, width)]
-        picked = pick(place, rows, source, half, capacity, which, first, width)
-        landed = [picked[0].reshape(capacity, PH, PW, width)]
-        for r in range(1, half):
-            pairs = [(d, d // half * half + (d % half ^ r)) for d in range(devices)]
-            moved = lax.ppermute(picked[r], "dec", pairs)
-            landed.append(moved.reshape(capacity, PH, PW, width))
-        return landed
+        landed = {}
+        for partners in partner_sets(half):
+            picked = pick(place, rows, sources, capacity, which, partners)
+            for r, array in zip(partners, picked):
+                if r > 0:
+                    pairs = [(d, d // half * half + (d % half ^ r)) for d in range(devices)]
+                    array = lax.ppermute(array, "dec", pairs)
+                landed[r] = array.reshape(capacity, PH, PW, width)
+        return [landed[r] for r in range(half)]
 
     tail = [taken_cells(), *(v.reshape(1, C_OUT) for v in (conv_bias, norm_gain, norm_shift))]
     scalars = (tile_count, place, fills)
-    own = exchange(panels, 0, 0, channels)
+    own = exchange(parts, 0)
     weights = stage(conv_weight)
     partial = None
     for n, (first, width) in enumerate(zip(firsts, SPLIT)):
-        brought = exchange(far[n], 1, 0, width)
+        brought = exchange([far[n]], 1)
         plan = (half, capacity, paired, (len(own), len(brought)))
         partial = conv_step(
             plan, first, width, scalars, weights, [*own, *brought], partial,

time: 109 us -> 109 us (level)
  waiting for transfers between devices: 34.6 us -> 38.5 us
  Pallas kernels: 32.4 us -> 30.2 us
  local copies, waits for them, and re-layouts: 8.19 us -> 6.08 us
    ppermute x23, waiting for transfers between devices: 27.3 us -> 31.3 us  [the longest x21 27.3 us: exchange(): array = lax.ppermute(array, 'dec', pairs)]
    pallas_call x3, Pallas kernels: 7.76 us -> 5.42 us  [pick(): pl.pallas_call(functools.partial(pick_kernel, capacity, which, partners,...]
    unnamed x12 -> x10, local copies, waits for them, and re-layouts: 4.24 us -> 3.02 us
  transfers between devices with their start and end apart: 24 -> 24, of which waited for: 9 -> 8; matrix products, arithmetic and copies ran while one was open for 3% -> 2% of each run, Pallas kernels for 18% -> 16%
where the time goes in v3:
time: 109 us
  waiting for transfers between devices  38.5 us (35%)
  starting transfers between devices  33.1 us (30%)
  Pallas kernels  30.2 us (28%)
  local copies, waits for them, and re-layouts  6.08 us (6%)
    ppermute x21, waiting for transfers between devices, exchange(): array = lax.ppermute(array, 'dec', pairs)  27.3 us
    ppermute x21, starting transfers between devices, exchange(): array = lax.ppermute(array, 'dec', pairs)  25.2 us
    pallas_call x2, Pallas kernels, conv_step(): pl.pallas_call(functools.partial(conv_kernel, plan, first, width, is_firs...  24.3 us
    all_to_all x1, waiting for transfers between devices, decode_tiles(): lax.all_to_all(sent, 'dec', 0, 0, tiled=True, axis_index_groups=halves)  7.27 us
    pallas_call x3, Pallas kernels, pick(): pl.pallas_call(functools.partial(pick_kernel, capacity, which, partners,...  5.42 us
    all_to_all x1, starting transfers between devices, decode_tiles(): lax.all_to_all(sent, 'dec', 0, 0, tiled=True, axis_index_groups=halves)  4.73 us
    ppermute x2, waiting for transfers between devices, decode_tiles(): far.append(lax.ppermute(part, 'dec', swap))  4.02 us
    ppermute x2, starting transfers between devices, decode_tiles(): far.append(lax.ppermute(part, 'dec', swap))  3.22 us
  transfers between devices with their start and end apart: 24, of which 8 were waited for; matrix products, arithmetic and copies ran while one was open for 2% of the time, Pallas kernels for 16%

profile of v3, /device:TPU:21, one launch (start us, length us, event | category | flops | bytes accessed | tf_op | source)
XLA Modules:
  0.0 109.2 jit_solution(1168693080082699732)
XLA Ops:
  0.0 1.3 %fusion.4 = (bf16[16,64,256]{2,1,0:T(8,128)(2,1)S(1)}, bf16[16,64,256]{2,1,0:T(8,128)(2,1)S(1)}) fusion(bf16[16,64,512]{2,1,0:T(8,128)(2,1)} %param.8), kind=kLoop, calls=%fused_computation.30 | loop fusion | bytes 2097152 | tf_op jit(solution)/shard_map/slice | solution.py:368
  4.1 4.7 %all-to-all-start = ((s32[8,2,4]{2,1,0:T(2,128)}), s32[8,2,4]{2,1,0:T(2,128)S(1)}, u32[]{:S(2)}, u32[]{:S(2)}) async-start(s32[8,2,4]{2,1,0:T(2,128)} %copy.20), calls=%async_computation | async-start | bytes 16384 | tf_op jit(solution)/shard_map/all_to_all | solution.py:365
  8.9 7.3 %all-to-all-done = s32[8,2,4]{2,1,0:T(2,128)S(1)} async-done(((s32[8,2,4]{2,1,0:T(2,128)}), s32[8,2,4]{2,1,0:T(2,128)S(1)}, u32[]{:S(2)}, u32[]{:S(2)}) %all-to-all-start) | async-done | bytes 288 | tf_op jit(solution)/shard_map/all_to_all | solution.py:365
  17.5 1.8 %collective-permute-start.5 = (bf16[4,64,512]{2,1,0:T(8,128)(2,1)S(1)}, bf16[4,64,512]{2,1,0:T(8,128)(2,1)S(1)}, u32[]{:S(2)}, u32[]{:S(2)}) collective-permute-start(bf16[4,64,512]{2,1,0:T(8,128)(2,1)S(1)} %get-tuple-element.37), channel_id=1, source_target_pairs={{0,6},{1,7},{2,4},{3,5},{4,2},{5,3},{6,0},{7,1},{8,14},{9,15},{10,... | collective-permute-start | bytes 786440 | tf_op jit(solution)/shard_map/ppermute | solution.py:392
  19.3 4.0 %collective-permute-done.7.refs_0_ = bf16[16,64,256]{2,1,0:T(8,128)(2,1)S(1)} collective-permute-done((bf16[16,64,256]{2,1,0:T(8,128)(2,1)S(1)}, bf16[16,64,256]{2,1,0:T(8,128)(2,1)S(1)}, u32[]{:S(2)}, u32[]{:S(2)}) %collective-permute-start.7) | collective-permute-done | bytes 524320 | tf_op jit(solution)/shard_map/ppermute | solution.py:373
  23.3 3.1 %collective-permute-start.8 = (bf16[16,64,256]{2,1,0:T(8,128)(2,1)S(1)}, bf16[16,64,256]{2,1,0:T(8,128)(2,1)S(1)}, u32[]{:S(2)}, u32[]{:S(2)}) collective-permute-start(bf16[16,64,256]{2,1,0:T(8,128)(2,1)S(1)} %get-tuple-element.39.refs_1_), channel_id=1, source_target_pairs={{0,8},{1,9},{2,10},{3,11},{4,12},{5,13},{6,14},{7,15},{8,0},{9,1},... | collective-permute-start | bytes 1572872 | tf_op jit(solution)/shard_map/ppermute | solution.py:373
  26.4 3.5 %collective-permute-start.6 = (bf16[4,64,512]{2,1,0:T(8,128)(2,1)S(1)}, bf16[4,64,512]{2,1,0:T(8,128)(2,1)S(1)}, u32[]{:S(2)}, u32[]{:S(2)}) collective-permute-start(bf16[4,64,512]{2,1,0:T(8,128)(2,1)S(1)} %get-tuple-element.38), channel_id=1, source_target_pairs={{0,7},{1,6},{2,5},{3,4},{4,3},{5,2},{6,1},{7,0},{8,15},{9,14},{10,... | collective-permute-start | bytes 786440 | tf_op jit(solution)/shard_map/ppermute | solution.py:392
  29.9 3.9 %collective-permute-done.4 = bf16[4,64,512]{2,1,0:T(8,128)(2,1)S(1)} collective-permute-done((bf16[4,64,512]{2,1,0:T(8,128)(2,1)S(1)}, bf16[4,64,512]{2,1,0:T(8,128)(2,1)S(1)}, u32[]{:S(2)}, u32[]{:S(2)}) %collective-permute-start.4) | collective-permute-done | bytes 262176 | tf_op jit(solution)/shard_map/ppermute | solution.py:392
  34.1 5.3 %collective-permute-done.5 = bf16[4,64,512]{2,1,0:T(8,128)(2,1)S(1)} collective-permute-done((bf16[4,64,512]{2,1,0:T(8,128)(2,1)S(1)}, bf16[4,64,512]{2,1,0:T(8,128)(2,1)S(1)}, u32[]{:S(2)}, u32[]{:S(2)}) %collective-permute-start.5) | collective-permute-done | bytes 262176 | tf_op jit(solution)/shard_map/ppermute | solution.py:392
  40.2 14.3 %collective-permute-done.6 = bf16[4,64,512]{2,1,0:T(8,128)(2,1)S(1)} collective-permute-done((bf16[4,64,512]{2,1,0:T(8,128)(2,1)S(1)}, bf16[4,64,512]{2,1,0:T(8,128)(2,1)S(1)}, u32[]{:S(2)}, u32[]{:S(2)}) %collective-permute-start.6) | collective-permute-done | bytes 262176 | tf_op jit(solution)/shard_map/ppermute | solution.py:392
  54.5 3.1 %collective-permute-start.3 = (bf16[4,64,512]{2,1,0:T(8,128)(2,1)S(1)}, bf16[4,64,512]{2,1,0:T(8,128)(2,1)S(1)}, u32[]{:S(2)}, u32[]{:S(2)}) collective-permute-start(bf16[4,64,512]{2,1,0:T(8,128)(2,1)S(1)} %get-tuple-element.35), channel_id=1, source_target_pairs={{0,4},{1,5},{2,6},{3,7},{4,0},{5,1},{6,2},{7,3},{8,12},{9,13},{10,... | collective-permute-start | bytes 786440 | tf_op jit(solution)/shard_map/ppermute | solution.py:392
  57.6 2.1 %pick.5 = (bf16[4,64,256]{2,1,0:T(8,128)(2,1)S(1)}, bf16[4,64,256]{2,1,0:T(8,128)(2,1)S(1)}, bf16[4,64,256]{2,1,0:T(8,128)(2,1)S(1)}, bf16[4,64,256]{2,1,0:T(8,1...) custom-call(s32[2]{0:T(128)S(1)} %pad_add_fusion.1.place.refs_1_, ...), custom_call_target="tpu_custom_call" | custom-call | tf_op jit(solution)/shard_map/pick/pallas_call | solution.py:71
  60.9 1.5 %collective-permute-start.18 = (bf16[4,64,256]{2,1,0:T(8,128)(2,1)S(1)}, bf16[4,64,256]{2,1,0:T(8,128)(2,1)S(1)}, u32[]{:S(2)}, u32[]{:S(2)}) collective-permute-start(bf16[4,64,256]{2,1,0:T(8,128)(2,1)S(1)} %get-tuple-element.52), channel_id=1, source_target_pairs={{0,3},{1,2},{2,1},{3,0},{4,7},{5,6},{6,5},{7,4},{8,11},{9,10},{10,... | collective-permute-start | bytes 393224 | tf_op jit(solution)/shard_map/ppermute | solution.py:392
  62.3 3.0 %copy-done = bf16[3,3,3,512,256]{4,3,2,1,0:T(8,128)(2,1)S(1)} copy-done((bf16[3,3,3,512,256]{4,3,2,1,0:T(8,128)(2,1)S(1)}, bf16[3,3,3,512,256]{4,3,2,1,0:T(8,128)(2,1)}, u32[]{:S(2)}) %copy-start) | copy-done | bytes 7077912
  65.8 2.1 %pick.4 = (bf16[4,64,256]{2,1,0:T(8,128)(2,1)S(1)}, bf16[4,64,256]{2,1,0:T(8,128)(2,1)S(1)}, bf16[4,64,256]{2,1,0:T(8,128)(2,1)S(1)}, bf16[4,64,256]{2,1,0:T(8,1...) custom-call(s32[2]{0:T(128)S(1)} %pad_add_fusion.1.place.refs_1_, ...), custom_call_target="tpu_custom_call" | custom-call | tf_op jit(solution)/shard_map/pick/pallas_call | solution.py:71
  68.0 1.8 %collective-permute-start.20 = (bf16[4,64,256]{2,1,0:T(8,128)(2,1)S(1)}, bf16[4,64,256]{2,1,0:T(8,128)(2,1)S(1)}, u32[]{:S(2)}, u32[]{:S(2)}) collective-permute-start(bf16[4,64,256]{2,1,0:T(8,128)(2,1)S(1)} %get-tuple-element.54), channel_id=1, source_target_pairs={{0,5},{1,4},{2,7},{3,6},{4,1},{5,0},{6,3},{7,2},{8,13},{9,12},{10,... | collective-permute-start | bytes 393224 | tf_op jit(solution)/shard_map/ppermute | solution.py:392
  69.8 2.6 %collective-permute-start.22 = (bf16[4,64,256]{2,1,0:T(8,128)(2,1)S(1)}, bf16[4,64,256]{2,1,0:T(8,128)(2,1)S(1)}, u32[]{:S(2)}, u32[]{:S(2)}) collective-permute-start(bf16[4,64,256]{2,1,0:T(8,128)(2,1)S(1)} %get-tuple-element.56), channel_id=1, source_target_pairs={{0,7},{1,6},{2,5},{3,4},{4,3},{5,2},{6,1},{7,0},{8,15},{9,14},{10,... | collective-permute-start | bytes 393224 | tf_op jit(solution)/shard_map/ppermute | solution.py:392
  72.9 1.3 %collective-permute-done.20 = bf16[4,64,256]{2,1,0:T(8,128)(2,1)S(1)} collective-permute-done((bf16[4,64,256]{2,1,0:T(8,128)(2,1)S(1)}, bf16[4,64,256]{2,1,0:T(8,128)(2,1)S(1)}, u32[]{:S(2)}, u32[]{:S(2)}) %collective-permute-start.20) | collective-permute-done | bytes 131104 | tf_op jit(solution)/shard_map/ppermute | solution.py:392
  74.7 1.3 %collective-permute-done.21 = bf16[4,64,256]{2,1,0:T(8,128)(2,1)S(1)} collective-permute-done((bf16[4,64,256]{2,1,0:T(8,128)(2,1)S(1)}, bf16[4,64,256]{2,1,0:T(8,128)(2,1)S(1)}, u32[]{:S(2)}, u32[]{:S(2)}) %collective-permute-start.21) | collective-permute-done | bytes 131104 | tf_op jit(solution)/shard_map/ppermute | solution.py:392
  76.0 1.9 %collective-permute-start.12 = (bf16[4,64,256]{2,1,0:T(8,128)(2,1)S(1)}, bf16[4,64,256]{2,1,0:T(8,128)(2,1)S(1)}, u32[]{:S(2)}, u32[]{:S(2)}) collective-permute-start(bf16[4,64,256]{2,1,0:T(8,128)(2,1)S(1)} %get-tuple-element.44), channel_id=1, source_target_pairs={{0,4},{1,5},{2,6},{3,7},{4,0},{5,1},{6,2},{7,3},{8,12},{9,13},{10,... | collective-permute-start | bytes 393224 | tf_op jit(solution)/shard_map/ppermute | solution.py:392
  79.0 2.0 %collective-permute-start.13 = (bf16[4,64,256]{2,1,0:T(8,128)(2,1)S(1)}, bf16[4,64,256]{2,1,0:T(8,128)(2,1)S(1)}, u32[]{:S(2)}, u32[]{:S(2)}) collective-permute-start(bf16[4,64,256]{2,1,0:T(8,128)(2,1)S(1)} %get-tuple-element.45), channel_id=1, source_target_pairs={{0,5},{1,4},{2,7},{3,6},{4,1},{5,0},{6,3},{7,2},{8,13},{9,12},{10,... | collective-permute-start | bytes 393224 | tf_op jit(solution)/shard_map/ppermute | solution.py:392
  81.9 2.9 %collective-permute-start.15 = (bf16[4,64,256]{2,1,0:T(8,128)(2,1)S(1)}, bf16[4,64,256]{2,1,0:T(8,128)(2,1)S(1)}, u32[]{:S(2)}, u32[]{:S(2)}) collective-permute-start(bf16[4,64,256]{2,1,0:T(8,128)(2,1)S(1)} %get-tuple-element.47), channel_id=1, source_target_pairs={{0,7},{1,6},{2,5},{3,4},{4,3},{5,2},{6,1},{7,0},{8,15},{9,14},{10,... | collective-permute-start | bytes 393224 | tf_op jit(solution)/shard_map/ppermute | solution.py:392
  84.8 11.0 %conv_part.1.refs_20_ = f32[4,448,256]{2,1,0:T(8,128)S(1)} custom-call(s32[1]{0:T(128)} %copy.21.refs_0_, s32[2]{0:T(128)S(1)} %pad_add_fusion.1.place.refs_1_, s32[64]{0:T(128)S(1)} %fusion.3.refs_2_, bf16[3,3,3,512,256]{4,3,2,1,0:T(8,128)(2,1)S(1)} %stage.1.refs_3_, bf16[4,8,8,512]{3,2,1,0:T(8,128)(2,1)S(1)} %bitcast.33, ...), custom_call_target="tpu_custom_call" | custom-call | flops 6341787648 | tf_op jit(solution)/shard_map/conv_part/pallas_call | solution.py:332
  96.0 13.3 %conv_last.1 = bf16[4,392,256]{2,1,0:T(8,128)(2,1)} custom-call(s32[1]{0:T(128)} %copy.21.refs_0_, s32[2]{0:T(128)S(1)} %pad_add_fusion.1.place.refs_1_, s32[64]{0:T(128)S(1)} %fusion.3.refs_2_, bf16[3,3,3,512,256]{4,3,2,1,0:T(8,128)(2,1)S(1)} %stage.1.refs_3_, bf16[4,8,8,512]{3,2,1,0:T(8,128)(2,1)S(1)} %bitcast.34, bf16[4,8,8,512]{3,2,1,0:T(8,128)(2,1)S(1)} %bitcast.42, ...), custom_call_target="tpu_custom_call" | custom-call | flops 6341787648 | tf_op jit(solution)/shard_map/conv_last/pallas_call | solution.py:332
  (56 shorter events, 9.1 us)
Async XLA Ops:
  1.3 22.0 %collective-permute-start.7 = (bf16[16,64,256]{2,1,0:T(8,128)(2,1)S(1)}, bf16[16,64,256]{2,1,0:T(8,128)(2,1)S(1)}, u32[]{:S(2)}, u32[]{:S(2)}) collective-permute-start(bf16[16,64,256]{2,1,0:T(8,128)(2,1)S(1)} %get-tuple-element.58.refs_0_), channel_id=1, source_target_pairs={{0,8},{1,9},{2,10},{3,11},{4,12},{5,13},{6,14},{7,15},{8,0},{9,1},... | collective-permute-start | bytes 1572872 | tf_op jit(solution)/shard_map/ppermute | solution.py:373
  4.1 12.1 %all-to-all-start = ((s32[8,2,4]{2,1,0:T(2,128)}), s32[8,2,4]{2,1,0:T(2,128)S(1)}, u32[]{:S(2)}, u32[]{:S(2)}) async-start(s32[8,2,4]{2,1,0:T(2,128)} %copy.20), calls=%async_computation | async-start | bytes 16384 | tf_op jit(solution)/shard_map/all_to_all | solution.py:365
  17.4 16.3 %collective-permute-start.4 = (bf16[4,64,512]{2,1,0:T(8,128)(2,1)S(1)}, bf16[4,64,512]{2,1,0:T(8,128)(2,1)S(1)}, u32[]{:S(2)}, u32[]{:S(2)}) collective-permute-start(bf16[4,64,512]{2,1,0:T(8,128)(2,1)S(1)} %get-tuple-element.36), channel_id=1, source_target_pairs={{0,5},{1,4},{2,7},{3,6},{4,1},{5,0},{6,3},{7,2},{8,13},{9,12},{10,... | collective-permute-start | bytes 786440 | tf_op jit(solution)/shard_map/ppermute | solution.py:392
  17.5 21.9 %collective-permute-start.5 = (bf16[4,64,512]{2,1,0:T(8,128)(2,1)S(1)}, bf16[4,64,512]{2,1,0:T(8,128)(2,1)S(1)}, u32[]{:S(2)}, u32[]{:S(2)}) collective-permute-start(bf16[4,64,512]{2,1,0:T(8,128)(2,1)S(1)} %get-tuple-element.37), channel_id=1, source_target_pairs={{0,6},{1,7},{2,4},{3,5},{4,2},{5,3},{6,0},{7,1},{8,14},{9,15},{10,... | collective-permute-start | bytes 786440 | tf_op jit(solution)/shard_map/ppermute | solution.py:392
  23.3 39.0 %collective-permute-start.8 = (bf16[16,64,256]{2,1,0:T(8,128)(2,1)S(1)}, bf16[16,64,256]{2,1,0:T(8,128)(2,1)S(1)}, u32[]{:S(2)}, u32[]{:S(2)}) collective-permute-start(bf16[16,64,256]{2,1,0:T(8,128)(2,1)S(1)} %get-tuple-element.39.refs_1_), channel_id=1, source_target_pairs={{0,8},{1,9},{2,10},{3,11},{4,12},{5,13},{6,14},{7,15},{8,0},{9,1},... | collective-permute-start | bytes 1572872 | tf_op jit(solution)/shard_map/ppermute | solution.py:373
  26.4 28.1 %collective-permute-start.6 = (bf16[4,64,512]{2,1,0:T(8,128)(2,1)S(1)}, bf16[4,64,512]{2,1,0:T(8,128)(2,1)S(1)}, u32[]{:S(2)}, u32[]{:S(2)}) collective-permute-start(bf16[4,64,512]{2,1,0:T(8,128)(2,1)S(1)} %get-tuple-element.38), channel_id=1, source_target_pairs={{0,7},{1,6},{2,5},{3,4},{4,3},{5,2},{6,1},{7,0},{8,15},{9,14},{10,... | collective-permute-start | bytes 786440 | tf_op jit(solution)/shard_map/ppermute | solution.py:392
  29.9 29.9 %collective-permute-start = (bf16[4,64,512]{2,1,0:T(8,128)(2,1)S(1)}, bf16[4,64,512]{2,1,0:T(8,128)(2,1)S(1)}, u32[]{:S(2)}, u32[]{:S(2)}) collective-permute-start(bf16[4,64,512]{2,1,0:T(8,128)(2,1)S(1)} %get-tuple-element.32), channel_id=1, source_target_pairs={{0,1},{1,0},{2,3},{3,2},{4,5},{5,4},{6,7},{7,6},{8,9},{9,8},{10,11... | collective-permute-start | bytes 786440 | tf_op jit(solution)/shard_map/ppermute | solution.py:392
  33.8 26.8 %collective-permute-start.1 = (bf16[4,64,512]{2,1,0:T(8,128)(2,1)S(1)}, bf16[4,64,512]{2,1,0:T(8,128)(2,1)S(1)}, u32[]{:S(2)}, u32[]{:S(2)}) collective-permute-start(bf16[4,64,512]{2,1,0:T(8,128)(2,1)S(1)} %get-tuple-element.33), channel_id=1, source_target_pairs={{0,2},{1,3},{2,0},{3,1},{4,6},{5,7},{6,4},{7,5},{8,10},{9,11},{10,... | collective-permute-start | bytes 786440 | tf_op jit(solution)/shard_map/ppermute | solution.py:392
  39.4 21.4 %collective-permute-start.2 = (bf16[4,64,512]{2,1,0:T(8,128)(2,1)S(1)}, bf16[4,64,512]{2,1,0:T(8,128)(2,1)S(1)}, u32[]{:S(2)}, u32[]{:S(2)}) collective-permute-start(bf16[4,64,512]{2,1,0:T(8,128)(2,1)S(1)} %get-tuple-element.34), channel_id=1, source_target_pairs={{0,3},{1,2},{2,1},{3,0},{4,7},{5,6},{6,5},{7,4},{8,11},{9,10},{10,... | collective-permute-start | bytes 786440 | tf_op jit(solution)/shard_map/ppermute | solution.py:392
  54.5 13.5 %collective-permute-start.3 = (bf16[4,64,512]{2,1,0:T(8,128)(2,1)S(1)}, bf16[4,64,512]{2,1,0:T(8,128)(2,1)S(1)}, u32[]{:S(2)}, u32[]{:S(2)}) collective-permute-start(bf16[4,64,512]{2,1,0:T(8,128)(2,1)S(1)} %get-tuple-element.35), channel_id=1, source_target_pairs={{0,4},{1,5},{2,6},{3,7},{4,0},{5,1},{6,2},{7,3},{8,12},{9,13},{10,... | collective-permute-start | bytes 786440 | tf_op jit(solution)/shard_map/ppermute | solution.py:392
  59.8 10.0 %collective-permute-start.16 = (bf16[4,64,256]{2,1,0:T(8,128)(2,1)S(1)}, bf16[4,64,256]{2,1,0:T(8,128)(2,1)S(1)}, u32[]{:S(2)}, u32[]{:S(2)}) collective-permute-start(bf16[4,64,256]{2,1,0:T(8,128)(2,1)S(1)} %get-tuple-element.50), channel_id=1, source_target_pairs={{0,1},{1,0},{2,3},{3,2},{4,5},{5,4},{6,7},{7,6},{8,9},{9,8},{10,11... | collective-permute-start | bytes 393224 | tf_op jit(solution)/shard_map/ppermute | solution.py:392
  60.6 9.2 %collective-permute-start.17 = (bf16[4,64,256]{2,1,0:T(8,128)(2,1)S(1)}, bf16[4,64,256]{2,1,0:T(8,128)(2,1)S(1)}, u32[]{:S(2)}, u32[]{:S(2)}) collective-permute-start(bf16[4,64,256]{2,1,0:T(8,128)(2,1)S(1)} %get-tuple-element.51), channel_id=1, source_target_pairs={{0,2},{1,3},{2,0},{3,1},{4,6},{5,7},{6,4},{7,5},{8,10},{9,11},{10,... | collective-permute-start | bytes 393224 | tf_op jit(solution)/shard_map/ppermute | solution.py:392
  60.9 11.6 %collective-permute-start.18 = (bf16[4,64,256]{2,1,0:T(8,128)(2,1)S(1)}, bf16[4,64,256]{2,1,0:T(8,128)(2,1)S(1)}, u32[]{:S(2)}, u32[]{:S(2)}) collective-permute-start(bf16[4,64,256]{2,1,0:T(8,128)(2,1)S(1)} %get-tuple-element.52), channel_id=1, source_target_pairs={{0,3},{1,2},{2,1},{3,0},{4,7},{5,6},{6,5},{7,4},{8,11},{9,10},{10,... | collective-permute-start | bytes 393224 | tf_op jit(solution)/shard_map/ppermute | solution.py:392
  62.3 10.3 %collective-permute-start.19 = (bf16[4,64,256]{2,1,0:T(8,128)(2,1)S(1)}, bf16[4,64,256]{2,1,0:T(8,128)(2,1)S(1)}, u32[]{:S(2)}, u32[]{:S(2)}) collective-permute-start(bf16[4,64,256]{2,1,0:T(8,128)(2,1)S(1)} %get-tuple-element.53), channel_id=1, source_target_pairs={{0,4},{1,5},{2,6},{3,7},{4,0},{5,1},{6,2},{7,3},{8,12},{9,13},{10,... | collective-permute-start | bytes 393224 | tf_op jit(solution)/shard_map/ppermute | solution.py:392
  68.0 6.2 %collective-permute-start.20 = (bf16[4,64,256]{2,1,0:T(8,128)(2,1)S(1)}, bf16[4,64,256]{2,1,0:T(8,128)(2,1)S(1)}, u32[]{:S(2)}, u32[]{:S(2)}) collective-permute-start(bf16[4,64,256]{2,1,0:T(8,128)(2,1)S(1)} %get-tuple-element.54), channel_id=1, source_target_pairs={{0,5},{1,4},{2,7},{3,6},{4,1},{5,0},{6,3},{7,2},{8,13},{9,12},{10,... | collective-permute-start | bytes 393224 | tf_op jit(solution)/shard_map/ppermute | solution.py:392
  69.8 6.1 %collective-permute-start.21 = (bf16[4,64,256]{2,1,0:T(8,128)(2,1)S(1)}, bf16[4,64,256]{2,1,0:T(8,128)(2,1)S(1)}, u32[]{:S(2)}, u32[]{:S(2)}) collective-permute-start(bf16[4,64,256]{2,1,0:T(8,128)(2,1)S(1)} %get-tuple-element.55), channel_id=1, source_target_pairs={{0,6},{1,7},{2,4},{3,5},{4,2},{5,3},{6,0},{7,1},{8,14},{9,15},{10,... | collective-permute-start | bytes 393224 | tf_op jit(solution)/shard_map/ppermute | solution.py:392
  69.8 9.2 %collective-permute-start.22 = (bf16[4,64,256]{2,1,0:T(8,128)(2,1)S(1)}, bf16[4,64,256]{2,1,0:T(8,128)(2,1)S(1)}, u32[]{:S(2)}, u32[]{:S(2)}) collective-permute-start(bf16[4,64,256]{2,1,0:T(8,128)(2,1)S(1)} %get-tuple-element.56), channel_id=1, source_target_pairs={{0,7},{1,6},{2,5},{3,4},{4,3},{5,2},{6,1},{7,0},{8,15},{9,14},{10,... | collective-permute-start | bytes 393224 | tf_op jit(solution)/shard_map/ppermute | solution.py:392
  72.5 8.6 %collective-permute-start.9 = (bf16[4,64,256]{2,1,0:T(8,128)(2,1)S(1)}, bf16[4,64,256]{2,1,0:T(8,128)(2,1)S(1)}, u32[]{:S(2)}, u32[]{:S(2)}) collective-permute-start(bf16[4,64,256]{2,1,0:T(8,128)(2,1)S(1)} %get-tuple-element.41), channel_id=1, source_target_pairs={{0,1},{1,0},{2,3},{3,2},{4,5},{5,4},{6,7},{7,6},{8,9},{9,8},{10,11... | collective-permute-start | bytes 393224 | tf_op jit(solution)/shard_map/ppermute | solution.py:392
  72.6 9.3 %collective-permute-start.10 = (bf16[4,64,256]{2,1,0:T(8,128)(2,1)S(1)}, bf16[4,64,256]{2,1,0:T(8,128)(2,1)S(1)}, u32[]{:S(2)}, u32[]{:S(2)}) collective-permute-start(bf16[4,64,256]{2,1,0:T(8,128)(2,1)S(1)} %get-tuple-element.42), channel_id=1, source_target_pairs={{0,2},{1,3},{2,0},{3,1},{4,6},{5,7},{6,4},{7,5},{8,10},{9,11},{10,... | collective-permute-start | bytes 393224 | tf_op jit(solution)/shard_map/ppermute | solution.py:392
  74.2 21.7 %collective-permute-start.11 = (bf16[4,64,256]{2,1,0:T(8,128)(2,1)S(1)}, bf16[4,64,256]{2,1,0:T(8,128)(2,1)S(1)}, u32[]{:S(2)}, u32[]{:S(2)}) collective-permute-start(bf16[4,64,256]{2,1,0:T(8,128)(2,1)S(1)} %get-tuple-element.43), channel_id=1, source_target_pairs={{0,3},{1,2},{2,1},{3,0},{4,7},{5,6},{6,5},{7,4},{8,11},{9,10},{10,... | collective-permute-start | bytes 393224 | tf_op jit(solution)/shard_map/ppermute | solution.py:392
  76.0 19.9 %collective-permute-start.12 = (bf16[4,64,256]{2,1,0:T(8,128)(2,1)S(1)}, bf16[4,64,256]{2,1,0:T(8,128)(2,1)S(1)}, u32[]{:S(2)}, u32[]{:S(2)}) collective-permute-start(bf16[4,64,256]{2,1,0:T(8,128)(2,1)S(1)} %get-tuple-element.44), channel_id=1, source_target_pairs={{0,4},{1,5},{2,6},{3,7},{4,0},{5,1},{6,2},{7,3},{8,12},{9,13},{10,... | collective-permute-start | bytes 393224 | tf_op jit(solution)/shard_map/ppermute | solution.py:392
  79.0 16.9 %collective-permute-start.13 = (bf16[4,64,256]{2,1,0:T(8,128)(2,1)S(1)}, bf16[4,64,256]{2,1,0:T(8,128)(2,1)S(1)}, u32[]{:S(2)}, u32[]{:S(2)}) collective-permute-start(bf16[4,64,256]{2,1,0:T(8,128)(2,1)S(1)} %get-tuple-element.45), channel_id=1, source_target_pairs={{0,5},{1,4},{2,7},{3,6},{4,1},{5,0},{6,3},{7,2},{8,13},{9,12},{10,... | collective-permute-start | bytes 393224 | tf_op jit(solution)/shard_map/ppermute | solution.py:392
  81.0 14.9 %collective-permute-start.14 = (bf16[4,64,256]{2,1,0:T(8,128)(2,1)S(1)}, bf16[4,64,256]{2,1,0:T(8,128)(2,1)S(1)}, u32[]{:S(2)}, u32[]{:S(2)}) collective-permute-start(bf16[4,64,256]{2,1,0:T(8,128)(2,1)S(1)} %get-tuple-element.46), channel_id=1, source_target_pairs={{0,6},{1,7},{2,4},{3,5},{4,2},{5,3},{6,0},{7,1},{8,14},{9,15},{10,... | collective-permute-start | bytes 393224 | tf_op jit(solution)/shard_map/ppermute | solution.py:392
  81.9 14.0 %collective-permute-start.15 = (bf16[4,64,256]{2,1,0:T(8,128)(2,1)S(1)}, bf16[4,64,256]{2,1,0:T(8,128)(2,1)S(1)}, u32[]{:S(2)}, u32[]{:S(2)}) collective-permute-start(bf16[4,64,256]{2,1,0:T(8,128)(2,1)S(1)} %get-tuple-element.47), channel_id=1, source_target_pairs={{0,7},{1,6},{2,5},{3,4},{4,3},{5,2},{6,1},{7,0},{8,15},{9,14},{10,... | collective-permute-start | bytes 393224 | tf_op jit(solution)/shard_map/ppermute | solution.py:392
  (5 other events, 47.5 us)

commit v4 on v3

--- a/solution.py
+++ b/solution.py
@@ -62,12 +62,30 @@
                         copy.wait()
 
 
+def copy_kernel(capacity, which, partners, place, rows, source, *outs):
+    for n, r in enumerate(partners):
+        q = place[1] ^ r
+        for k in range(capacity):
+            outs[n][k] = source[rows[(q * 2 + which) * capacity + k]]
+
+
 def pick(place, rows, sources, capacity, which, partners):
     cells = sources[0].shape[1]
     widths = [source.shape[2] for source in sources]
     columns = tuple((sum(widths[:n]), widths[n]) for n in range(len(widths)))
     smem = pl.BlockSpec(memory_space=pltpu.SMEM)
     shape = jax.ShapeDtypeStruct((capacity, cells, sum(widths)), jnp.bfloat16)
+    if len(sources) == 1:
+        vmem = pl.BlockSpec(memory_space=pltpu.VMEM)
+        return pl.pallas_call(
+            functools.partial(copy_kernel, capacity, which, partners),
+            out_shape=[shape] * len(partners),
+            in_specs=[smem, smem, vmem],
+            out_specs=[vmem] * len(partners),
+            compiler_params=pltpu.CompilerParams(vmem_limit_bytes=8 * 2**20),
+            cost_estimate=pl.CostEstimate(flops=0, bytes_accessed=0, transcendentals=0),
+            name="pick_far",
+        )(place, rows, *sources)
     return pl.pallas_call(
         functools.partial(pick_kernel, capacity, which, partners, columns),
         out_shape=[shape] * len(partners),
@@ -365,7 +383,10 @@
     got = lax.all_to_all(sent, "dec", 0, 0, tiled=True, axis_index_groups=halves)
 
     firsts = [sum(SPLIT[:n]) for n in range(len(SPLIT))]
-    parts = [panels[:, :, first : first + width] for first, width in zip(firsts, SPLIT)]
+    parts = []
+    for n, (first, width) in enumerate(zip(firsts, SPLIT)):
+        whole = lax.optimization_barrier(panels) if n else panels
+        parts.append(whole[:, :, first : first + width])
     far = []
     for part in parts:
         if far:

time: 109 us -> 107 us (0.982)
  Pallas kernels: 30.2 us -> 27.2 us
    pallas_call x3 -> x1, Pallas kernels: 5.42 us -> 1.14 us  [pick(): pl.pallas_call(functools.partial(pick_kernel, capacity, which, partners,...]
    pallas_call x0 -> x2, Pallas kernels: none -> 1.24 us  [pick(): pl.pallas_call(functools.partial(copy_kernel, capacity, which, partners),...]
  transfers between devices with their start and end apart: 24 -> 24, of which waited for: 8 -> 9; matrix products, arithmetic and copies ran while one was open for 2% -> 3% of each run, Pallas kernels for 16% -> 13%
where the time goes in v4:
time: 107 us; the launch traced here: 106 us
  waiting for transfers between devices  38.3 us (36%)
  starting transfers between devices  32.6 us (30%)
  Pallas kernels  27.2 us (25%)
  local copies, waits for them, and re-layouts  6.97 us (7%)
    ppermute x21, waiting for transfers between devices, exchange(): array = lax.ppermute(array, 'dec', pairs)  28.1 us
    ppermute x21, starting transfers between devices, exchange(): array = lax.ppermute(array, 'dec', pairs)  24.7 us
    pallas_call x2, Pallas kernels, conv_step(): pl.pallas_call(functools.partial(conv_kernel, plan, first, width, is_firs...  24.3 us
    all_to_all x1, waiting for transfers between devices, decode_tiles(): lax.all_to_all(sent, 'dec', 0, 0, tiled=True, axis_index_groups=halves)  6.19 us
    all_to_all x1, starting transfers between devices, decode_tiles(): lax.all_to_all(sent, 'dec', 0, 0, tiled=True, axis_index_groups=halves)  4.73 us
    ppermute x2, waiting for transfers between devices, decode_tiles(): far.append(lax.ppermute(part, 'dec', swap))  4.02 us
    ppermute x2, starting transfers between devices, decode_tiles(): far.append(lax.ppermute(part, 'dec', swap))  3.22 us
    unnamed x10, local copies, waits for them, and re-layouts  3.02 us
  transfers between devices with their start and end apart: 24, of which 9 were waited for; matrix products, arithmetic and copies ran while one was open for 3% of the time, Pallas kernels for 13%

profile of v4, /device:TPU:21, one launch (start us, length us, event | category | flops | bytes accessed | tf_op | source)
XLA Modules:
  0.0 106.3 jit_solution(5083529044268346591)
XLA Ops:
  0.0 1.1 %slice.6.refs_0_ = bf16[16,64,256]{2,1,0:T(8,128)(2,1)S(1)} slice(bf16[16,64,512]{2,1,0:T(8,128)(2,1)} %param.8), slice={[0:16], [0:64], [0:256]} | slice | bytes 1048576 | tf_op jit(solution)/shard_map/slice | solution.py:389
  3.9 4.7 %all-to-all-start = ((s32[8,2,4]{2,1,0:T(2,128)}), s32[8,2,4]{2,1,0:T(2,128)S(1)}, u32[]{:S(2)}, u32[]{:S(2)}) async-start(s32[8,2,4]{2,1,0:T(2,128)} %copy.20), calls=%async_computation | async-start | bytes 16384 | tf_op jit(solution)/shard_map/all_to_all | solution.py:383
  9.8 6.2 %all-to-all-done = s32[8,2,4]{2,1,0:T(2,128)S(1)} async-done(((s32[8,2,4]{2,1,0:T(2,128)}), s32[8,2,4]{2,1,0:T(2,128)S(1)}, u32[]{:S(2)}, u32[]{:S(2)}) %all-to-all-start) | async-done | bytes 288 | tf_op jit(solution)/shard_map/all_to_all | solution.py:383
  16.1 1.1 %pick.1 = (bf16[4,64,512]{2,1,0:T(8,128)(2,1)S(1)}, bf16[4,64,512]{2,1,0:T(8,128)(2,1)S(1)}, bf16[4,64,512]{2,1,0:T(8,128)(2,1)S(1)}, bf16[4,64,512]{2,1,0:T(8,1...) custom-call(s32[2]{0:T(128)S(1)} %pad_add_fusion.1.place.refs_1_, ...), custom_call_target="tpu_custom_call" | custom-call | tf_op jit(solution)/shard_map/pick/pallas_call | solution.py:89
  17.3 1.8 %collective-permute-start.5 = (bf16[4,64,512]{2,1,0:T(8,128)(2,1)S(1)}, bf16[4,64,512]{2,1,0:T(8,128)(2,1)S(1)}, u32[]{:S(2)}, u32[]{:S(2)}) collective-permute-start(bf16[4,64,512]{2,1,0:T(8,128)(2,1)S(1)} %get-tuple-element.37), channel_id=1, source_target_pairs={{0,6},{1,7},{2,4},{3,5},{4,2},{5,3},{6,0},{7,1},{8,14},{9,15},{10,... | collective-permute-start | bytes 786440 | tf_op jit(solution)/shard_map/ppermute | solution.py:413
  19.1 4.0 %collective-permute-done.7.source = bf16[16,64,256]{2,1,0:T(8,128)(2,1)S(1)} collective-permute-done((bf16[16,64,256]{2,1,0:T(8,128)(2,1)S(1)}, bf16[16,64,256]{2,1,0:T(8,128)(2,1)S(1)}, u32[]{:S(2)}, u32[]{:S(2)}) %collective-permute-start.7) | collective-permute-done | bytes 524320 | tf_op jit(solution)/shard_map/ppermute | solution.py:394
  23.1 3.1 %collective-permute-start.8 = (bf16[16,64,256]{2,1,0:T(8,128)(2,1)S(1)}, bf16[16,64,256]{2,1,0:T(8,128)(2,1)S(1)}, u32[]{:S(2)}, u32[]{:S(2)}) collective-permute-start(bf16[16,64,256]{2,1,0:T(8,128)(2,1)S(1)} %slice.8.refs_1_), channel_id=1, source_target_pairs={{0,8},{1,9},{2,10},{3,11},{4,12},{5,13},{6,14},{7,15},{8,0},{9,1},... | collective-permute-start | bytes 1572872 | tf_op jit(solution)/shard_map/ppermute | solution.py:394
  26.2 3.5 %collective-permute-start.6 = (bf16[4,64,512]{2,1,0:T(8,128)(2,1)S(1)}, bf16[4,64,512]{2,1,0:T(8,128)(2,1)S(1)}, u32[]{:S(2)}, u32[]{:S(2)}) collective-permute-start(bf16[4,64,512]{2,1,0:T(8,128)(2,1)S(1)} %get-tuple-element.38), channel_id=1, source_target_pairs={{0,7},{1,6},{2,5},{3,4},{4,3},{5,2},{6,1},{7,0},{8,15},{9,14},{10,... | collective-permute-start | bytes 786440 | tf_op jit(solution)/shard_map/ppermute | solution.py:413
  29.7 3.9 %collective-permute-done.4 = bf16[4,64,512]{2,1,0:T(8,128)(2,1)S(1)} collective-permute-done((bf16[4,64,512]{2,1,0:T(8,128)(2,1)S(1)}, bf16[4,64,512]{2,1,0:T(8,128)(2,1)S(1)}, u32[]{:S(2)}, u32[]{:S(2)}) %collective-permute-start.4) | collective-permute-done | bytes 262176 | tf_op jit(solution)/shard_map/ppermute | solution.py:413
  34.0 5.3 %collective-permute-done.5 = bf16[4,64,512]{2,1,0:T(8,128)(2,1)S(1)} collective-permute-done((bf16[4,64,512]{2,1,0:T(8,128)(2,1)S(1)}, bf16[4,64,512]{2,1,0:T(8,128)(2,1)S(1)}, u32[]{:S(2)}, u32[]{:S(2)}) %collective-permute-start.5) | collective-permute-done | bytes 262176 | tf_op jit(solution)/shard_map/ppermute | solution.py:413
  40.0 14.3 %collective-permute-done.6 = bf16[4,64,512]{2,1,0:T(8,128)(2,1)S(1)} collective-permute-done((bf16[4,64,512]{2,1,0:T(8,128)(2,1)S(1)}, bf16[4,64,512]{2,1,0:T(8,128)(2,1)S(1)}, u32[]{:S(2)}, u32[]{:S(2)}) %collective-permute-start.6) | collective-permute-done | bytes 262176 | tf_op jit(solution)/shard_map/ppermute | solution.py:413
  54.3 3.1 %collective-permute-start.3 = (bf16[4,64,512]{2,1,0:T(8,128)(2,1)S(1)}, bf16[4,64,512]{2,1,0:T(8,128)(2,1)S(1)}, u32[]{:S(2)}, u32[]{:S(2)}) collective-permute-start(bf16[4,64,512]{2,1,0:T(8,128)(2,1)S(1)} %get-tuple-element.35), channel_id=1, source_target_pairs={{0,4},{1,5},{2,6},{3,7},{4,0},{5,1},{6,2},{7,3},{8,12},{9,13},{10,... | collective-permute-start | bytes 786440 | tf_op jit(solution)/shard_map/ppermute | solution.py:413
  59.1 1.5 %collective-permute-start.18 = (bf16[4,64,256]{2,1,0:T(8,128)(2,1)S(1)}, bf16[4,64,256]{2,1,0:T(8,128)(2,1)S(1)}, u32[]{:S(2)}, u32[]{:S(2)}) collective-permute-start(bf16[4,64,256]{2,1,0:T(8,128)(2,1)S(1)} %get-tuple-element.52), channel_id=1, source_target_pairs={{0,3},{1,2},{2,1},{3,0},{4,7},{5,6},{6,5},{7,4},{8,11},{9,10},{10,... | collective-permute-start | bytes 393224 | tf_op jit(solution)/shard_map/ppermute | solution.py:413
  60.6 3.0 %copy-done = bf16[3,3,3,512,256]{4,3,2,1,0:T(8,128)(2,1)S(1)} copy-done((bf16[3,3,3,512,256]{4,3,2,1,0:T(8,128)(2,1)S(1)}, bf16[3,3,3,512,256]{4,3,2,1,0:T(8,128)(2,1)}, u32[]{:S(2)}) %copy-start) | copy-done | bytes 7077912
  64.8 2.2 %collective-permute-start.20 = (bf16[4,64,256]{2,1,0:T(8,128)(2,1)S(1)}, bf16[4,64,256]{2,1,0:T(8,128)(2,1)S(1)}, u32[]{:S(2)}, u32[]{:S(2)}) collective-permute-start(bf16[4,64,256]{2,1,0:T(8,128)(2,1)S(1)} %get-tuple-element.54), channel_id=1, source_target_pairs={{0,5},{1,4},{2,7},{3,6},{4,1},{5,0},{6,3},{7,2},{8,13},{9,12},{10,... | collective-permute-start | bytes 393224 | tf_op jit(solution)/shard_map/ppermute | solution.py:413
  67.0 2.2 %collective-permute-start.22 = (bf16[4,64,256]{2,1,0:T(8,128)(2,1)S(1)}, bf16[4,64,256]{2,1,0:T(8,128)(2,1)S(1)}, u32[]{:S(2)}, u32[]{:S(2)}) collective-permute-start(bf16[4,64,256]{2,1,0:T(8,128)(2,1)S(1)} %get-tuple-element.56), channel_id=1, source_target_pairs={{0,7},{1,6},{2,5},{3,4},{4,3},{5,2},{6,1},{7,0},{8,15},{9,14},{10,... | collective-permute-start | bytes 393224 | tf_op jit(solution)/shard_map/ppermute | solution.py:413
  70.0 1.3 %collective-permute-done.20 = bf16[4,64,256]{2,1,0:T(8,128)(2,1)S(1)} collective-permute-done((bf16[4,64,256]{2,1,0:T(8,128)(2,1)S(1)}, bf16[4,64,256]{2,1,0:T(8,128)(2,1)S(1)}, u32[]{:S(2)}, u32[]{:S(2)}) %collective-permute-start.20) | collective-permute-done | bytes 131104 | tf_op jit(solution)/shard_map/ppermute | solution.py:413
  71.5 1.9 %collective-permute-done.21 = bf16[4,64,256]{2,1,0:T(8,128)(2,1)S(1)} collective-permute-done((bf16[4,64,256]{2,1,0:T(8,128)(2,1)S(1)}, bf16[4,64,256]{2,1,0:T(8,128)(2,1)S(1)}, u32[]{:S(2)}, u32[]{:S(2)}) %collective-permute-start.21) | collective-permute-done | bytes 131104 | tf_op jit(solution)/shard_map/ppermute | solution.py:413
  73.4 1.7 %collective-permute-start.12 = (bf16[4,64,256]{2,1,0:T(8,128)(2,1)S(1)}, bf16[4,64,256]{2,1,0:T(8,128)(2,1)S(1)}, u32[]{:S(2)}, u32[]{:S(2)}) collective-permute-start(bf16[4,64,256]{2,1,0:T(8,128)(2,1)S(1)} %get-tuple-element.44), channel_id=1, source_target_pairs={{0,4},{1,5},{2,6},{3,7},{4,0},{5,1},{6,2},{7,3},{8,12},{9,13},{10,... | collective-permute-start | bytes 393224 | tf_op jit(solution)/shard_map/ppermute | solution.py:413
  75.1 1.1 %collective-permute-done.22 = bf16[4,64,256]{2,1,0:T(8,128)(2,1)S(1)} collective-permute-done((bf16[4,64,256]{2,1,0:T(8,128)(2,1)S(1)}, bf16[4,64,256]{2,1,0:T(8,128)(2,1)S(1)}, u32[]{:S(2)}, u32[]{:S(2)}) %collective-permute-start.22) | collective-permute-done | bytes 131104 | tf_op jit(solution)/shard_map/ppermute | solution.py:413
  76.2 2.1 %collective-permute-start.13 = (bf16[4,64,256]{2,1,0:T(8,128)(2,1)S(1)}, bf16[4,64,256]{2,1,0:T(8,128)(2,1)S(1)}, u32[]{:S(2)}, u32[]{:S(2)}) collective-permute-start(bf16[4,64,256]{2,1,0:T(8,128)(2,1)S(1)} %get-tuple-element.45), channel_id=1, source_target_pairs={{0,5},{1,4},{2,7},{3,6},{4,1},{5,0},{6,3},{7,2},{8,13},{9,12},{10,... | collective-permute-start | bytes 393224 | tf_op jit(solution)/shard_map/ppermute | solution.py:413
  79.1 2.8 %collective-permute-start.15 = (bf16[4,64,256]{2,1,0:T(8,128)(2,1)S(1)}, bf16[4,64,256]{2,1,0:T(8,128)(2,1)S(1)}, u32[]{:S(2)}, u32[]{:S(2)}) collective-permute-start(bf16[4,64,256]{2,1,0:T(8,128)(2,1)S(1)} %get-tuple-element.47), channel_id=1, source_target_pairs={{0,7},{1,6},{2,5},{3,4},{4,3},{5,2},{6,1},{7,0},{8,15},{9,14},{10,... | collective-permute-start | bytes 393224 | tf_op jit(solution)/shard_map/ppermute | solution.py:413
  81.9 11.0 %conv_part.1.refs_20_ = f32[4,448,256]{2,1,0:T(8,128)S(1)} custom-call(s32[1]{0:T(128)} %copy.21.refs_0_, s32[2]{0:T(128)S(1)} %pad_add_fusion.1.place.refs_1_, s32[64]{0:T(128)S(1)} %fusion.3.refs_2_, bf16[3,3,3,512,256]{4,3,2,1,0:T(8,128)(2,1)S(1)} %stage.1.refs_3_, bf16[4,8,8,512]{3,2,1,0:T(8,128)(2,1)S(1)} %bitcast.33, ...), custom_call_target="tpu_custom_call" | custom-call | flops 6341787648 | tf_op jit(solution)/shard_map/conv_part/pallas_call | solution.py:350
  93.1 13.3 %conv_last.1 = bf16[4,392,256]{2,1,0:T(8,128)(2,1)} custom-call(s32[1]{0:T(128)} %copy.21.refs_0_, s32[2]{0:T(128)S(1)} %pad_add_fusion.1.place.refs_1_, s32[64]{0:T(128)S(1)} %fusion.3.refs_2_, bf16[3,3,3,512,256]{4,3,2,1,0:T(8,128)(2,1)S(1)} %stage.1.refs_3_, bf16[4,8,8,512]{3,2,1,0:T(8,128)(2,1)S(1)} %bitcast.34, bf16[4,8,8,512]{3,2,1,0:T(8,128)(2,1)S(1)} %bitcast.42, ...), custom_call_target="tpu_custom_call" | custom-call | flops 6341787648 | tf_op jit(solution)/shard_map/conv_last/pallas_call | solution.py:350
  (57 shorter events, 9.1 us)
Async XLA Ops:
  1.1 22.0 %collective-permute-start.7 = (bf16[16,64,256]{2,1,0:T(8,128)(2,1)S(1)}, bf16[16,64,256]{2,1,0:T(8,128)(2,1)S(1)}, u32[]{:S(2)}, u32[]{:S(2)}) collective-permute-start(bf16[16,64,256]{2,1,0:T(8,128)(2,1)S(1)} %slice.6.refs_0_), channel_id=1, source_target_pairs={{0,8},{1,9},{2,10},{3,11},{4,12},{5,13},{6,14},{7,15},{8,0},{9,1},... | collective-permute-start | bytes 1572872 | tf_op jit(solution)/shard_map/ppermute | solution.py:394
  3.9 12.1 %all-to-all-start = ((s32[8,2,4]{2,1,0:T(2,128)}), s32[8,2,4]{2,1,0:T(2,128)S(1)}, u32[]{:S(2)}, u32[]{:S(2)}) async-start(s32[8,2,4]{2,1,0:T(2,128)} %copy.20), calls=%async_computation | async-start | bytes 16384 | tf_op jit(solution)/shard_map/all_to_all | solution.py:383
  17.2 16.3 %collective-permute-start.4 = (bf16[4,64,512]{2,1,0:T(8,128)(2,1)S(1)}, bf16[4,64,512]{2,1,0:T(8,128)(2,1)S(1)}, u32[]{:S(2)}, u32[]{:S(2)}) collective-permute-start(bf16[4,64,512]{2,1,0:T(8,128)(2,1)S(1)} %get-tuple-element.36), channel_id=1, source_target_pairs={{0,5},{1,4},{2,7},{3,6},{4,1},{5,0},{6,3},{7,2},{8,13},{9,12},{10,... | collective-permute-start | bytes 786440 | tf_op jit(solution)/shard_map/ppermute | solution.py:413
  17.3 21.9 %collective-permute-start.5 = (bf16[4,64,512]{2,1,0:T(8,128)(2,1)S(1)}, bf16[4,64,512]{2,1,0:T(8,128)(2,1)S(1)}, u32[]{:S(2)}, u32[]{:S(2)}) collective-permute-start(bf16[4,64,512]{2,1,0:T(8,128)(2,1)S(1)} %get-tuple-element.37), channel_id=1, source_target_pairs={{0,6},{1,7},{2,4},{3,5},{4,2},{5,3},{6,0},{7,1},{8,14},{9,15},{10,... | collective-permute-start | bytes 786440 | tf_op jit(solution)/shard_map/ppermute | solution.py:413
  23.1 37.5 %collective-permute-start.8 = (bf16[16,64,256]{2,1,0:T(8,128)(2,1)S(1)}, bf16[16,64,256]{2,1,0:T(8,128)(2,1)S(1)}, u32[]{:S(2)}, u32[]{:S(2)}) collective-permute-start(bf16[16,64,256]{2,1,0:T(8,128)(2,1)S(1)} %slice.8.refs_1_), channel_id=1, source_target_pairs={{0,8},{1,9},{2,10},{3,11},{4,12},{5,13},{6,14},{7,15},{8,0},{9,1},... | collective-permute-start | bytes 1572872 | tf_op jit(solution)/shard_map/ppermute | solution.py:394
  26.2 28.1 %collective-permute-start.6 = (bf16[4,64,512]{2,1,0:T(8,128)(2,1)S(1)}, bf16[4,64,512]{2,1,0:T(8,128)(2,1)S(1)}, u32[]{:S(2)}, u32[]{:S(2)}) collective-permute-start(bf16[4,64,512]{2,1,0:T(8,128)(2,1)S(1)} %get-tuple-element.38), channel_id=1, source_target_pairs={{0,7},{1,6},{2,5},{3,4},{4,3},{5,2},{6,1},{7,0},{8,15},{9,14},{10,... | collective-permute-start | bytes 786440 | tf_op jit(solution)/shard_map/ppermute | solution.py:413
  29.7 28.4 %collective-permute-start = (bf16[4,64,512]{2,1,0:T(8,128)(2,1)S(1)}, bf16[4,64,512]{2,1,0:T(8,128)(2,1)S(1)}, u32[]{:S(2)}, u32[]{:S(2)}) collective-permute-start(bf16[4,64,512]{2,1,0:T(8,128)(2,1)S(1)} %get-tuple-element.32), channel_id=1, source_target_pairs={{0,1},{1,0},{2,3},{3,2},{4,5},{5,4},{6,7},{7,6},{8,9},{9,8},{10,11... | collective-permute-start | bytes 786440 | tf_op jit(solution)/shard_map/ppermute | solution.py:413
  33.6 25.3 %collective-permute-start.1 = (bf16[4,64,512]{2,1,0:T(8,128)(2,1)S(1)}, bf16[4,64,512]{2,1,0:T(8,128)(2,1)S(1)}, u32[]{:S(2)}, u32[]{:S(2)}) collective-permute-start(bf16[4,64,512]{2,1,0:T(8,128)(2,1)S(1)} %get-tuple-element.33), channel_id=1, source_target_pairs={{0,2},{1,3},{2,0},{3,1},{4,6},{5,7},{6,4},{7,5},{8,10},{9,11},{10,... | collective-permute-start | bytes 786440 | tf_op jit(solution)/shard_map/ppermute | solution.py:413
  39.3 19.9 %collective-permute-start.2 = (bf16[4,64,512]{2,1,0:T(8,128)(2,1)S(1)}, bf16[4,64,512]{2,1,0:T(8,128)(2,1)S(1)}, u32[]{:S(2)}, u32[]{:S(2)}) collective-permute-start(bf16[4,64,512]{2,1,0:T(8,128)(2,1)S(1)} %get-tuple-element.34), channel_id=1, source_target_pairs={{0,3},{1,2},{2,1},{3,0},{4,7},{5,6},{6,5},{7,4},{8,11},{9,10},{10,... | collective-permute-start | bytes 786440 | tf_op jit(solution)/shard_map/ppermute | solution.py:413
  54.3 10.4 %collective-permute-start.3 = (bf16[4,64,512]{2,1,0:T(8,128)(2,1)S(1)}, bf16[4,64,512]{2,1,0:T(8,128)(2,1)S(1)}, u32[]{:S(2)}, u32[]{:S(2)}) collective-permute-start(bf16[4,64,512]{2,1,0:T(8,128)(2,1)S(1)} %get-tuple-element.35), channel_id=1, source_target_pairs={{0,4},{1,5},{2,6},{3,7},{4,0},{5,1},{6,2},{7,3},{8,12},{9,13},{10,... | collective-permute-start | bytes 786440 | tf_op jit(solution)/shard_map/ppermute | solution.py:413
  58.1 8.9 %collective-permute-start.16 = (bf16[4,64,256]{2,1,0:T(8,128)(2,1)S(1)}, bf16[4,64,256]{2,1,0:T(8,128)(2,1)S(1)}, u32[]{:S(2)}, u32[]{:S(2)}) collective-permute-start(bf16[4,64,256]{2,1,0:T(8,128)(2,1)S(1)} %get-tuple-element.50), channel_id=1, source_target_pairs={{0,1},{1,0},{2,3},{3,2},{4,5},{5,4},{6,7},{7,6},{8,9},{9,8},{10,11... | collective-permute-start | bytes 393224 | tf_op jit(solution)/shard_map/ppermute | solution.py:413
  58.9 8.1 %collective-permute-start.17 = (bf16[4,64,256]{2,1,0:T(8,128)(2,1)S(1)}, bf16[4,64,256]{2,1,0:T(8,128)(2,1)S(1)}, u32[]{:S(2)}, u32[]{:S(2)}) collective-permute-start(bf16[4,64,256]{2,1,0:T(8,128)(2,1)S(1)} %get-tuple-element.51), channel_id=1, source_target_pairs={{0,2},{1,3},{2,0},{3,1},{4,6},{5,7},{6,4},{7,5},{8,10},{9,11},{10,... | collective-permute-start | bytes 393224 | tf_op jit(solution)/shard_map/ppermute | solution.py:413
  59.1 10.1 %collective-permute-start.18 = (bf16[4,64,256]{2,1,0:T(8,128)(2,1)S(1)}, bf16[4,64,256]{2,1,0:T(8,128)(2,1)S(1)}, u32[]{:S(2)}, u32[]{:S(2)}) collective-permute-start(bf16[4,64,256]{2,1,0:T(8,128)(2,1)S(1)} %get-tuple-element.52), channel_id=1, source_target_pairs={{0,3},{1,2},{2,1},{3,0},{4,7},{5,6},{6,5},{7,4},{8,11},{9,10},{10,... | collective-permute-start | bytes 393224 | tf_op jit(solution)/shard_map/ppermute | solution.py:413
  60.6 9.1 %collective-permute-start.19 = (bf16[4,64,256]{2,1,0:T(8,128)(2,1)S(1)}, bf16[4,64,256]{2,1,0:T(8,128)(2,1)S(1)}, u32[]{:S(2)}, u32[]{:S(2)}) collective-permute-start(bf16[4,64,256]{2,1,0:T(8,128)(2,1)S(1)} %get-tuple-element.53), channel_id=1, source_target_pairs={{0,4},{1,5},{2,6},{3,7},{4,0},{5,1},{6,2},{7,3},{8,12},{9,13},{10,... | collective-permute-start | bytes 393224 | tf_op jit(solution)/shard_map/ppermute | solution.py:413
  64.8 6.6 %collective-permute-start.20 = (bf16[4,64,256]{2,1,0:T(8,128)(2,1)S(1)}, bf16[4,64,256]{2,1,0:T(8,128)(2,1)S(1)}, u32[]{:S(2)}, u32[]{:S(2)}) collective-permute-start(bf16[4,64,256]{2,1,0:T(8,128)(2,1)S(1)} %get-tuple-element.54), channel_id=1, source_target_pairs={{0,5},{1,4},{2,7},{3,6},{4,1},{5,0},{6,3},{7,2},{8,13},{9,12},{10,... | collective-permute-start | bytes 393224 | tf_op jit(solution)/shard_map/ppermute | solution.py:413
  67.0 6.4 %collective-permute-start.21 = (bf16[4,64,256]{2,1,0:T(8,128)(2,1)S(1)}, bf16[4,64,256]{2,1,0:T(8,128)(2,1)S(1)}, u32[]{:S(2)}, u32[]{:S(2)}) collective-permute-start(bf16[4,64,256]{2,1,0:T(8,128)(2,1)S(1)} %get-tuple-element.55), channel_id=1, source_target_pairs={{0,6},{1,7},{2,4},{3,5},{4,2},{5,3},{6,0},{7,1},{8,14},{9,15},{10,... | collective-permute-start | bytes 393224 | tf_op jit(solution)/shard_map/ppermute | solution.py:413
  67.0 9.3 %collective-permute-start.22 = (bf16[4,64,256]{2,1,0:T(8,128)(2,1)S(1)}, bf16[4,64,256]{2,1,0:T(8,128)(2,1)S(1)}, u32[]{:S(2)}, u32[]{:S(2)}) collective-permute-start(bf16[4,64,256]{2,1,0:T(8,128)(2,1)S(1)} %get-tuple-element.56), channel_id=1, source_target_pairs={{0,7},{1,6},{2,5},{3,4},{4,3},{5,2},{6,1},{7,0},{8,15},{9,14},{10,... | collective-permute-start | bytes 393224 | tf_op jit(solution)/shard_map/ppermute | solution.py:413
  69.2 9.1 %collective-permute-start.9 = (bf16[4,64,256]{2,1,0:T(8,128)(2,1)S(1)}, bf16[4,64,256]{2,1,0:T(8,128)(2,1)S(1)}, u32[]{:S(2)}, u32[]{:S(2)}) collective-permute-start(bf16[4,64,256]{2,1,0:T(8,128)(2,1)S(1)} %get-tuple-element.41), channel_id=1, source_target_pairs={{0,1},{1,0},{2,3},{3,2},{4,5},{5,4},{6,7},{7,6},{8,9},{9,8},{10,11... | collective-permute-start | bytes 393224 | tf_op jit(solution)/shard_map/ppermute | solution.py:413
  69.7 9.3 %collective-permute-start.10 = (bf16[4,64,256]{2,1,0:T(8,128)(2,1)S(1)}, bf16[4,64,256]{2,1,0:T(8,128)(2,1)S(1)}, u32[]{:S(2)}, u32[]{:S(2)}) collective-permute-start(bf16[4,64,256]{2,1,0:T(8,128)(2,1)S(1)} %get-tuple-element.42), channel_id=1, source_target_pairs={{0,2},{1,3},{2,0},{3,1},{4,6},{5,7},{6,4},{7,5},{8,10},{9,11},{10,... | collective-permute-start | bytes 393224 | tf_op jit(solution)/shard_map/ppermute | solution.py:413
  71.3 21.7 %collective-permute-start.11 = (bf16[4,64,256]{2,1,0:T(8,128)(2,1)S(1)}, bf16[4,64,256]{2,1,0:T(8,128)(2,1)S(1)}, u32[]{:S(2)}, u32[]{:S(2)}) collective-permute-start(bf16[4,64,256]{2,1,0:T(8,128)(2,1)S(1)} %get-tuple-element.43), channel_id=1, source_target_pairs={{0,3},{1,2},{2,1},{3,0},{4,7},{5,6},{6,5},{7,4},{8,11},{9,10},{10,... | collective-permute-start | bytes 393224 | tf_op jit(solution)/shard_map/ppermute | solution.py:413
  73.4 19.6 %collective-permute-start.12 = (bf16[4,64,256]{2,1,0:T(8,128)(2,1)S(1)}, bf16[4,64,256]{2,1,0:T(8,128)(2,1)S(1)}, u32[]{:S(2)}, u32[]{:S(2)}) collective-permute-start(bf16[4,64,256]{2,1,0:T(8,128)(2,1)S(1)} %get-tuple-element.44), channel_id=1, source_target_pairs={{0,4},{1,5},{2,6},{3,7},{4,0},{5,1},{6,2},{7,3},{8,12},{9,13},{10,... | collective-permute-start | bytes 393224 | tf_op jit(solution)/shard_map/ppermute | solution.py:413
  76.2 16.8 %collective-permute-start.13 = (bf16[4,64,256]{2,1,0:T(8,128)(2,1)S(1)}, bf16[4,64,256]{2,1,0:T(8,128)(2,1)S(1)}, u32[]{:S(2)}, u32[]{:S(2)}) collective-permute-start(bf16[4,64,256]{2,1,0:T(8,128)(2,1)S(1)} %get-tuple-element.45), channel_id=1, source_target_pairs={{0,5},{1,4},{2,7},{3,6},{4,1},{5,0},{6,3},{7,2},{8,13},{9,12},{10,... | collective-permute-start | bytes 393224 | tf_op jit(solution)/shard_map/ppermute | solution.py:413
  78.4 14.7 %collective-permute-start.14 = (bf16[4,64,256]{2,1,0:T(8,128)(2,1)S(1)}, bf16[4,64,256]{2,1,0:T(8,128)(2,1)S(1)}, u32[]{:S(2)}, u32[]{:S(2)}) collective-permute-start(bf16[4,64,256]{2,1,0:T(8,128)(2,1)S(1)} %get-tuple-element.46), channel_id=1, source_target_pairs={{0,6},{1,7},{2,4},{3,5},{4,2},{5,3},{6,0},{7,1},{8,14},{9,15},{10,... | collective-permute-start | bytes 393224 | tf_op jit(solution)/shard_map/ppermute | solution.py:413
  79.1 13.9 %collective-permute-start.15 = (bf16[4,64,256]{2,1,0:T(8,128)(2,1)S(1)}, bf16[4,64,256]{2,1,0:T(8,128)(2,1)S(1)}, u32[]{:S(2)}, u32[]{:S(2)}) collective-permute-start(bf16[4,64,256]{2,1,0:T(8,128)(2,1)S(1)} %get-tuple-element.47), channel_id=1, source_target_pairs={{0,7},{1,6},{2,5},{3,4},{4,3},{5,2},{6,1},{7,0},{8,15},{9,14},{10,... | collective-permute-start | bytes 393224 | tf_op jit(solution)/shard_map/ppermute | solution.py:413
  (5 other events, 47.5 us)
